TPU v7x, 1024 devices: a whole 4x8x16 slice. The times are simulated.
1024 devices in a mesh: row: 16 (over y, core), col: 16 (over z), layer: 4 (over x).
Axes of the slice: x: 4, y: 8, z: 16, core: 2. Of those that a mesh axis runs over, the one named last changes fastest.
Arguments:
- a_panel: bfloat16 [8, 8192, 1024], P('layer', 'row', 'col'), may hold values from -6 to 6
- b_panel: bfloat16 [8, 1024, 16384], P('layer', 'row', 'col'), may hold values from -0.1875 to 0.1875
- a_mask: int32 [8, 128, 16], P('layer', 'row', 'col'), may hold values from 0 to 1, as said below
- b_mask: int32 [8, 16, 256], P('layer', 'row', 'col'), may hold values from 0 to 1, as said below
- c_pattern: int32 [128, 256], P(('row', 'layer'), 'col'), may hold values from 0 to 1, as said below
Outputs:
- filtered: float32 [8192, 16384], P(('row', 'layer'), 'col')
Inputs may be any that keep to these rules, and one draw needn't show every extreme that they name: `a_mask`: 1 marks a nonzero block; in every step, every block column and every aligned group of 8 block rows holds at most 2 ones, and some such group holds exactly 2. `b_mask`: 1 marks a nonzero block; in every step, every block row and every aligned group of 16 block columns holds at most 4 ones, and some such group holds exactly 4. `c_pattern`: 1 marks a kept block.
All inputs are finite; a program needn't handle non-finite values.
Results may differ from a plain program's by a relative error of at most 0.0003.
Values may be sent and summed in bfloat16 or wider, within the bound.
No kernel may reach another device: no remote copies, remote signals or barrier semaphores. Data moves between devices by JAX's collectives and lax.ppermute only.
A program may use at most 64 MiB of HBM per device.

v0:
```python
import jax
import jax.numpy as jnp
from jax import lax
from jax.sharding import PartitionSpec as P

BS = 64


def spread(mask, width):
    lead = mask.shape[:-2]
    first, second = (mask.shape[-2], mask.shape[-1])
    grown = jnp.broadcast_to(mask[..., :, None, :, None], lead + (first, width, second, width))
    return grown.reshape(lead + (first * width, second * width))


def body(a_panel, b_panel, a_mask, b_mask, c_pattern):
    a_live = a_panel * spread(a_mask.astype(jnp.bfloat16), BS)
    b_live = b_panel * spread(b_mask.astype(jnp.bfloat16), BS)
    b_whole = lax.all_gather(b_live, "row", axis=1, tiled=True)
    a_whole = lax.all_gather(a_live, "col", axis=2, tiled=True)
    product = lax.psum_scatter(
        jnp.einsum("sik,skj->ij", a_whole, b_whole, preferred_element_type=jnp.float32),
        "layer",
        scatter_dimension=0,
        tiled=True,
    )
    return product * spread(c_pattern.astype(jnp.float32), BS)


def solution(mesh):
    in_specs = (
        P("layer", "row", "col"),
        P("layer", "row", "col"),
        P("layer", "row", "col"),
        P("layer", "row", "col"),
        P(("row", "layer"), "col"),
    )
    out_specs = P(("row", "layer"), "col")
    return jax.shard_map(body, mesh=mesh, in_specs=in_specs, out_specs=out_specs, check_vma=False)
```

profile of v0, /device:TPU:1, one launch (start us, length us, event | category | flops | bytes accessed | tf_op | source)
XLA Modules:
  0.0 199.3 jit_solution(913230804226637953)
XLA Ops:
  6.5 0.0 all-gather.3.cloned.1.call-start
  6.5 0.7 convert_element_type.9
  7.2 0.1 broadcast_in_dim.31
  7.3 0.1 broadcast_in_dim.32
  7.4 1.6 broadcast_multiply_fusion.1
  9.0 0.0 all-gather.3.cloned.1.call-update
  9.0 0.0 all-gather.5.cloned.1.call-start
  9.0 0.7 convert_element_type.10
  9.7 0.1 broadcast_in_dim.35
  9.8 0.1 broadcast_in_dim.36
  9.9 1.7 broadcast_multiply_fusion
  11.6 0.0 all-gather.5.cloned.1.call-update
  11.6 0.0 reduce-scatter.2.cloned.1.call-start
  11.6 75.3 %all-gather.3.cloned.1.call-done = bf16[2,512,1024]{1,2,0:T(8,128)(2,1)} async-done(((bf16[2,512,64]{1,2,0:T(8,128)(2,1)}), bf16[2,512,1024]{1,2,0:T(8,128)(2,1)}) %all-gather.3.cloned.1.call-update) | async-done | bytes 2097168 | tf_op jit(solution)/shard_map/all_gather | solution.py:20
  86.9 58.2 %all-gather.5.cloned.1.call-done = bf16[2,1024,1024]{2,1,0:T(8,128)(2,1)} async-done(((bf16[2,64,1024]{2,1,0:T(8,128)(2,1)}), bf16[2,1024,1024]{2,1,0:T(8,128)(2,1)}) %all-gather.5.cloned.1.call-update) | async-done | bytes 4194320 | tf_op jit(solution)/shard_map/all_gather | solution.py:19
  145.1 6.5 %convolution_bitcast_fusion = f32[512,1024]{1,0:T(8,128)} fusion(bf16[2,512,1024]{1,2,0:T(8,128)(2,1)} %all-gather.3.cloned.1.call-done, bf16[2,1024,1024]{2,1,0:T(8,128)(2,1)} %all-gather.5.cloned.1.call-done), kind=kOutput, calls=%fused_computation | convolution fusion | flops 2147483648 | bytes 8388608 | tf_op jit(solution)/shard_map/sik,skj->ij/dot_general | solution.py:22
  151.6 0.0 copy-start
  151.6 0.0 reduce-scatter.2.cloned.1.call-update
  151.6 0.7 copy-done
  152.3 0.1 broadcast_in_dim.38
  152.4 0.3 reshape.14
  152.7 38.2 %reduce-scatter.2.cloned.1.call-done = f32[128,1024]{1,0:T(8,128)} async-done(((f32[512,1024]{1,0:T(8,128)}), f32[128,1024]{1,0:T(8,128)}) %reduce-scatter.2.cloned.1.call-update) | async-done | bytes 524304 | tf_op jit(solution)/shard_map/reduce_scatter | solution.py:21
  190.9 1.9 mul.11
  (3 shorter events, 0.0 us)
Async XLA Ops:
  6.5 80.4 %all-gather.3.cloned.1.call-start = ((), (), s32[]{:S(2)}) async-start(), calls=%async_computation.1 | async-start | bytes 2228224 | tf_op jit(solution)/shard_map/all_gather | solution.py:20
  9.0 136.1 %all-gather.5.cloned.1.call-start = ((), (), s32[]{:S(2)}) async-start(), calls=%async_computation.2 | async-start | bytes 4456448 | tf_op jit(solution)/shard_map/all_gather | solution.py:19
  11.6 179.3 %reduce-scatter.2.cloned.1.call-start = ((), (), s32[]{:S(2)}) async-start(), calls=%async_computation.3 | async-start | bytes 2621440 | tf_op jit(solution)/shard_map/reduce_scatter | solution.py:21
  151.6 0.7 copy-start
Sparse Core Ops, SparseCore 0:
  10.0 76.8 all-gather.2
  89.6 55.3 all-gather.4
  151.7 39.1 reduce-scatter.1
where the time goes:
time: 200 us; the launch traced here: 199 us
  waiting for transfers between devices  172 us (86%)
  between operations  13.1 us (7%)
  matrix products  6.53 us (3%)
  other arithmetic  6.5 us (3%)
    all_gather x1, waiting for transfers between devices, body(): a_whole = lax.all_gather(a_live, 'col', axis=2, tiled=True)  75.3 us
    all_gather x1, waiting for transfers between devices, body(): b_whole = lax.all_gather(b_live, 'row', axis=1, tiled=True)  58.2 us
    reduce_scatter x1, waiting for transfers between devices, body(): lax.psum_scatter(jnp.einsum('sik,skj->ij', a_whole, b_whole, preferred_el...  38.2 us
    dot_general x1, matrix products, body(): jnp.einsum('sik,skj->ij', a_whole, b_whole, preferred_element_type=jnp.fl...  6.53 us
  transfers between devices with their start and end apart: 3, of which 3 were waited for; matrix products, arithmetic and copies ran while one was open for 1% of the time, Pallas kernels for 0%

commit v1 on v0

v1 whole, which is shorter than its diff:
```python
import functools

import jax
import jax.numpy as jnp
from jax import lax
from jax.experimental import pallas as pl
from jax.experimental.pallas import tpu as pltpu
from jax.sharding import PartitionSpec as P

BS = 64
BR = 8
BC = 16
KB = 16
MOSTA = 2
MOSTB = 4
STEPS = 2
LAYERS = 4
NONE = 100
EXTRA = 8

F32, BF16, I32, I16 = jnp.float32, jnp.bfloat16, jnp.int32, jnp.int16
SMEM = pl.BlockSpec(memory_space=pltpu.SMEM)
VMEM = pl.BlockSpec(memory_space=pltpu.VMEM)


def grant(mib):
    return pltpu.CompilerParams(vmem_limit_bytes=mib * 2**20)


def lanes(rows=1):
    return lax.broadcasted_iota(I32, (rows, 128), 1)


def halves(left, right, rows=1):
    return jnp.where(lanes(rows) < BS, left, right)


def slot_ids(bits, most):
    ids = [jnp.int32(NONE)] * most
    seen = jnp.int32(0)
    for i, bit in enumerate(bits):
        one = bit != 0
        for s in range(most):
            ids[s] = jnp.where(one & (seen == s), jnp.int32(i), ids[s])
        seen = seen + one.astype(I32)
    return ids


def swap_halves(x):
    return pltpu.roll(x, BS, 1)


def compact(panel, pairs, ids):
    outs = [jnp.zeros((BS, 128), F32) for _ in range(len(ids) // 2)]
    for p in range(pairs):
        straight = panel(p)
        turned = swap_halves(straight)
        for o in range(len(outs)):
            want = halves(ids[2 * o], ids[2 * o + 1], BS)
            outs[o] = jnp.where(want == halves(2 * p, 2 * p + 1, BS), straight, outs[o])
            outs[o] = jnp.where(want == halves(2 * p + 1, 2 * p, BS), turned, outs[o])
    return outs


def pack_a_kernel(mask, at, out):
    ids = [slot_ids([mask[s, i] for i in range(BR)], MOSTA) for s in range(STEPS)]
    steps = [
        compact(lambda p: at[s, :, 128 * p : 128 * p + 128].astype(F32), BR // 2, ids[s])[0]
        for s in range(STEPS)
    ]
    body = jnp.concatenate(steps, axis=0).T.astype(BF16)
    row = lax.broadcasted_iota(I32, (EXTRA, 128), 0)
    index = jnp.where(
        row == 0,
        halves(ids[0][0], ids[1][0], EXTRA),
        halves(ids[0][1], ids[1][1], EXTRA),
    )
    index = index.astype(F32).astype(BF16)
    for d in range(out.shape[0]):
        out[d, 0:128, :] = body
        out[d, 128 : 128 + EXTRA, :] = index


def pack_b_kernel(mask, b, out):
    row = lax.broadcasted_iota(I32, (EXTRA, 128), 0)
    ids = [slot_ids([mask[s, j] for j in range(BC)], MOSTB) for s in range(STEPS)]
    for s in range(STEPS):
        pair = compact(lambda p: b[s, :, 128 * p : 128 * p + 128].astype(F32), BC // 2, ids[s])
        for o in range(2):
            out[BS * s : BS * s + BS, 128 * o : 128 * o + 128] = pair[o].astype(BF16)
    for o in range(2):
        index = jnp.where(
            row == 0,
            halves(ids[0][2 * o], ids[0][2 * o + 1], EXTRA),
            halves(ids[1][2 * o], ids[1][2 * o + 1], EXTRA),
        )
        out[128 : 128 + EXTRA, 128 * o : 128 * o + 128] = index.astype(F32).astype(BF16)


def spread_b_kernel(core, own, other, out):
    odd = core[0]

    def chunk(source, y, place):
        index = source[y, 128 : 128 + EXTRA, :].astype(F32)
        parts = []
        for o in range(2):
            straight = index[:, 128 * o : 128 * o + 128]
            parts += [straight, swap_halves(straight)]
        for s in range(STEPS):
            data = []
            for o in range(2):
                half = source[y, BS * s : BS * s + BS, 128 * o : 128 * o + 128]
                data += [half, swap_halves(half.astype(F32)).astype(BF16)]
            for p in range(BC // 2):
                target = halves(2 * p, 2 * p + 1, EXTRA).astype(F32)
                total = None
                for part, values in zip(parts, data):
                    chosen = jnp.where(part == target, 1.0, 0.0)[s : s + 1].astype(BF16)
                    term = values * chosen
                    total = term if total is None else total + term
                out[place, BS * s : BS * s + BS, 128 * p : 128 * p + 128] = total

    def step(y, carry):
        chunk(own, y, 2 * y + odd)
        chunk(other, y, 2 * y + 1 - odd)
        return carry

    lax.fori_loop(0, own.shape[0], step, 0)


def product_kernel(a, b, out, dense):
    @pl.when(pl.program_id(0) == 0)
    def _():
        for c in range(KB):
            index = a[c, 128 : 128 + EXTRA, :].astype(F32)
            for i in range(BR):
                total = None
                for s in range(MOSTA):
                    chosen = jnp.where(index == float(i), 1.0, 0.0)[s : s + 1].astype(BF16)
                    term = a[c, BS * s : BS * s + BS, :] * chosen
                    total = term if total is None else total + term
                dense[BS * i : BS * i + BS, 128 * c : 128 * c + 128] = total

    width = out.shape[2]
    rows = out.shape[1] - EXTRA
    right = b[...].reshape(KB * 128, width)
    total = jnp.dot(dense[...], right, preferred_element_type=F32)
    for l in range(LAYERS):
        part = total[rows * l : rows * l + rows]
        top = jnp.max(jnp.abs(part), axis=0, keepdims=True)
        power = jnp.floor(jnp.log2(jnp.maximum(top, 1e-30))) - 13.0
        out[l, 0:rows, :] = jnp.round(part * jnp.exp2(-power)).astype(I32).astype(I16)
        out[l, rows : rows + EXTRA, :] = jnp.broadcast_to(power, (EXTRA, width)).astype(I32).astype(I16)


def filter_kernel(parts, keep, out):
    rows = out.shape[0]
    total = None
    for l in range(LAYERS):
        power = parts[l, rows : rows + EXTRA, :].astype(I32).astype(F32)[0:1]
        term = parts[l, 0:rows, :].astype(I32).astype(F32) * jnp.exp2(power)
        total = term if total is None else total + term
    for i in range(rows // BS):
        out[BS * i : BS * i + BS, :] = total[BS * i : BS * i + BS] * keep[i : i + 1, :]


def body(a_panel, b_panel, a_mask, b_mask, c_pattern):
    core = lax.rem(lax.axis_index("row"), 2).astype(I32).reshape(1)
    a_sent = pl.pallas_call(
        pack_a_kernel,
        out_shape=jax.ShapeDtypeStruct((KB, 128 + EXTRA, 128), BF16),
        in_specs=[SMEM, VMEM],
        out_specs=VMEM,
        cost_estimate=pl.CostEstimate(flops=10**6, bytes_accessed=10**6, transcendentals=0),
        compiler_params=grant(4),
        name="pack_a",
    )(a_mask.reshape(STEPS, BR), jnp.swapaxes(a_panel, 1, 2))
    a_all = lax.all_to_all(a_sent, "col", 0, 0, tiled=True)
    b_sent = pl.pallas_call(
        pack_b_kernel,
        out_shape=jax.ShapeDtypeStruct((128 + EXTRA, 256), BF16),
        in_specs=[SMEM, VMEM],
        out_specs=VMEM,
        cost_estimate=pl.CostEstimate(flops=10**6, bytes_accessed=10**6, transcendentals=0),
        compiler_params=grant(4),
        name="pack_b",
    )(b_mask.reshape(STEPS, BC), b_panel)
    same_core = [[2 * y + c for y in range(8)] for c in range(2)]
    b_own = lax.all_gather(b_sent, "row", axis_index_groups=same_core)
    b_other = lax.ppermute(b_own, "row", [(r, r ^ 1) for r in range(16)])
    b_dense = pl.pallas_call(
        spread_b_kernel,
        out_shape=jax.ShapeDtypeStruct((KB, 128, 1024), BF16),
        in_specs=[SMEM, VMEM, VMEM],
        out_specs=VMEM,
        cost_estimate=pl.CostEstimate(flops=10**7, bytes_accessed=6 * 10**6, transcendentals=0),
        compiler_params=grant(12),
        name="spread_b",
    )(core, b_own, b_other)
    keep = jnp.repeat(c_pattern.astype(F32), BS, axis=1)
    width = 256
    sums = pl.pallas_call(
        product_kernel,
        out_shape=jax.ShapeDtypeStruct((LAYERS, 128 + EXTRA, 1024), I16),
        grid=(1024 // width,),
        in_specs=[
            pl.BlockSpec((KB, 128 + EXTRA, 128), lambda j: (0, 0, 0)),
            pl.BlockSpec((KB, 128, width), lambda j: (0, 0, j)),
        ],
        out_specs=pl.BlockSpec((LAYERS, 128 + EXTRA, width), lambda j: (0, 0, j)),
        scratch_shapes=[pltpu.VMEM((512, KB * 128), BF16)],
        cost_estimate=pl.CostEstimate(flops=2 * 10**9, bytes_accessed=6 * 10**6, transcendentals=0),
        compiler_params=grant(16),
        name="product",
    )(a_all, b_dense)
    parts = lax.all_to_all(sums, "layer", 0, 0, tiled=True)
    return pl.pallas_call(
        filter_kernel,
        out_shape=jax.ShapeDtypeStruct((128, 1024), F32),
        in_specs=[VMEM, VMEM],
        out_specs=VMEM,
        cost_estimate=pl.CostEstimate(flops=10**6, bytes_accessed=2 * 10**6, transcendentals=0),
        compiler_params=grant(8),
        name="filter",
    )(parts, keep)


def solution(mesh):
    spec = P("layer", "row", "col")
    out = P(("row", "layer"), "col")
    return jax.shard_map(
        body, mesh=mesh, in_specs=(spec, spec, spec, spec, out), out_specs=out, check_vma=False
    )
```

time: 200 us -> 88.5 us (0.44)
  waiting for transfers between devices: 172 us -> 16.6 us
  starting transfers between devices: 0.09 us -> 30.9 us
  blocking collectives: 0 us -> 22.5 us
  between operations: 13.1 us -> 0.07 us
  Pallas kernels: 0 us -> 12 us
  matrix products: 6.53 us -> 0 us
  other arithmetic: 6.5 us -> 0.01 us
  local copies, waits for them, and re-layouts: 1.44 us -> 5.93 us
    all_gather x2 -> x0, waiting for transfers between devices: 133 us -> none  [the longest x1 75.3 us: body(): a_whole = lax.all_gather(a_live, 'col', axis=2, tiled=True)]
    reduce_scatter x1 -> x0, waiting for transfers between devices: 38.2 us -> none  [body(): lax.psum_scatter(jnp.einsum('sik,skj->ij', a_whole, b_whole, preferred_el...]
    all_to_all x0 -> x2, starting transfers between devices: none -> 23.6 us  [the longest x1 19.4 us: body(): a_all = lax.all_to_all(a_sent, 'col', 0, 0, tiled=True)]
    all_gather x0 -> x1, blocking collectives: none -> 22.5 us  [body(): b_own = lax.all_gather(b_sent, 'row', axis_index_groups=same_core)]
    all_to_all x0 -> x2, waiting for transfers between devices: none -> 15.1 us  [the longest x1 15.1 us: body(): parts = lax.all_to_all(sums, 'layer', 0, 0, tiled=True)]
    pallas_call x0 -> x5, Pallas kernels: none -> 12 us  [the longest x1 5.08 us: body(): pl.pallas_call(product_kernel, out_shape=jax.ShapeDtypeStruct((LAYERS, 12...]
    ppermute x0 -> x1, starting transfers between devices: none -> 7.38 us  [body(): b_other = lax.ppermute(b_own, 'row', [(r, r ^ 1) for r in range(16)])]
    dot_general x1 -> x0, matrix products: 6.53 us -> none  [body(): jnp.einsum('sik,skj->ij', a_whole, b_whole, preferred_element_type=jnp.fl...]
  transfers between devices with their start and end apart: 3 -> 3, of which waited for: 3 -> 2; matrix products, arithmetic and copies ran while one was open for 1% -> 0% of each run, Pallas kernels for 0% -> 5%
where the time goes in v1:
time: 88.5 us; the launch traced here: 88.1 us
  starting transfers between devices  30.9 us (35%)
  blocking collectives  22.5 us (25%)
  waiting for transfers between devices  16.6 us (19%)
  Pallas kernels  12 us (14%)
  local copies, waits for them, and re-layouts  5.93 us (7%)
    all_gather x1, blocking collectives, body(): b_own = lax.all_gather(b_sent, 'row', axis_index_groups=same_core)  22.5 us
    all_to_all x1, starting transfers between devices, body(): a_all = lax.all_to_all(a_sent, 'col', 0, 0, tiled=True)  19.4 us
    all_to_all x1, waiting for transfers between devices, body(): parts = lax.all_to_all(sums, 'layer', 0, 0, tiled=True)  15.1 us
    ppermute x1, starting transfers between devices, body(): b_other = lax.ppermute(b_own, 'row', [(r, r ^ 1) for r in range(16)])  7.38 us
    unnamed x14, local copies, waits for them, and re-layouts  5.77 us
    pallas_call x1, Pallas kernels, body(): pl.pallas_call(product_kernel, out_shape=jax.ShapeDtypeStruct((LAYERS, 12...  5.08 us
    all_to_all x1, starting transfers between devices, body(): parts = lax.all_to_all(sums, 'layer', 0, 0, tiled=True)  4.14 us
    pallas_call x1, Pallas kernels, body(): pl.pallas_call(spread_b_kernel, out_shape=jax.ShapeDtypeStruct((KB, 128,...  3.53 us
  transfers between devices with their start and end apart: 3, of which 2 were waited for; matrix products, arithmetic and copies ran while one was open for 0% of the time, Pallas kernels for 5%

profile of v1, /device:TPU:1, one launch (start us, length us, event | category | flops | bytes accessed | tf_op | source)
XLA Modules:
  0.0 88.1 jit_solution(11495861789232982246)
XLA Ops:
  0.0 0.0 copy-start.2
  0.0 0.0 copy-start.3
  0.0 0.9 %copy-done.3 = bf16[2,512,64]{1,2,0:T(8,128)(2,1)S(1)} copy-done((bf16[2,512,64]{1,2,0:T(8,128)(2,1)S(1)}, bf16[2,512,64]{1,2,0:T(8,128)(2,1)}, u32[]{:S(2)}) %copy-start.3) | copy-done | bytes 131096
  1.0 0.7 copy-done.4
  1.6 1.5 %pack_a.1 = bf16[16,136,128]{2,1,0:T(8,128)(2,1)} custom-call(s32[2,8]{1,0:T(2,128)S(1)} %bitcast.8, bf16[2,64,512]{2,1,0:T(8,128)(2,1)S(1)} %bitcast.7), custom_call_target="tpu_custom_call" | custom-call | flops 1000000 | bytes 1000000 | tf_op jit(solution)/shard_map/pack_a/pallas_call | solution.py:169
  3.2 19.4 %all-to-all-start = ((bf16[16,136,128]{2,1,0:T(8,128)(2,1)}), bf16[16,136,128]{2,1,0:T(8,128)(2,1)S(1)}, u32[]{:S(2)}, u32[]{:S(2)}) async-start(bf16[16,136,128]{2,1,0:T(8,128)(2,1)} %pack_a.1), calls=%async_computation | async-start | bytes 1114112 | tf_op jit(solution)/shard_map/all_to_all | solution.py:178
  22.6 0.0 copy-done.2
  22.6 0.0 copy-done.5
  22.6 0.8 pack_b.1
  23.4 22.5 %all-gather = bf16[1088,256]{1,0:T(8,128)(2,1)S(1)} all-gather(bf16[136,256]{1,0:T(8,128)(2,1)S(1)} %pack_b.1), channel_id=2, replica_groups={{0,128,256,384,512,640,768,896},{64,192,320,448,576,704,832,960},{1,129..., dimensions={0}, use_global_device_ids=true | all-gather | bytes 626688 | tf_op jit(solution)/shard_map/all_gather | solution.py:189
  45.9 7.4 %collective-permute-start = (bf16[8,136,256]{2,1,0:T(8,128)(2,1)S(1)}, bf16[8,136,256]{2,1,0:T(8,128)(2,1)S(1)}, u32[]{:S(2)}, u32[]{:S(2)}) collective-permute-start(bf16[8,136,256]{2,1,0:T(8,128)(2,1)S(1)} %bitcast.5), channel_id=1, source_target_pairs={{0,64},{64,0},{128,192},{192,128},{256,320},{320,256},{384,448},{4... | collective-permute-start | bytes 1671176 | tf_op jit(solution)/shard_map/ppermute | solution.py:190
  53.3 1.6 %collective-permute-done.other = bf16[8,136,256]{2,1,0:T(8,128)(2,1)S(1)} collective-permute-done((bf16[8,136,256]{2,1,0:T(8,128)(2,1)S(1)}, bf16[8,136,256]{2,1,0:T(8,128)(2,1)S(1)}, u32[]{:S(2)}, u32[]{:S(2)}) %collective-permute-start) | collective-permute-done | bytes 557088 | tf_op jit(solution)/shard_map/ppermute | solution.py:190
  54.9 3.5 %spread_b.1.b = bf16[16,128,1024]{2,1,0:T(8,128)(2,1)S(1)} custom-call(s32[1]{0:T(128)} %bitcast.2.core, bf16[8,136,256]{2,1,0:T(8,128)(2,1)S(1)} %bitcast.6, bf16[8,136,256]{2,1,0:T(8,128)(2,1)S(1)} %collective-permute-done.other), custom_call_target="tpu_custom_call" | custom-call | flops 10000000 | bytes 6000000 | tf_op jit(solution)/shard_map/spread_b/pallas_call | solution.py:191
  58.4 0.0 copy-start
  58.4 1.9 %copy-done = bf16[16,128,1024]{2,1,0:T(8,128)(2,1)} copy-done((bf16[16,128,1024]{2,1,0:T(8,128)(2,1)}, bf16[16,128,1024]{2,1,0:T(8,128)(2,1)S(1)}, u32[]{:S(2)}) %copy-start) | copy-done | bytes 4194328
  60.3 0.0 all-to-all-done.a
  60.3 2.2 %copy-done.1 = bf16[16,128,1024]{2,1,0:T(8,128)(2,1)S(1)} copy-done((bf16[16,128,1024]{2,1,0:T(8,128)(2,1)S(1)}, bf16[16,128,1024]{2,1,0:T(8,128)(2,1)}, u32[]{:S(2)}) %copy-start.1) | copy-done | bytes 4194328
  62.5 5.1 %product.1 = s16[4,136,1024]{2,1,0:T(8,128)(2,1)} custom-call(bf16[16,136,128]{2,1,0:T(8,128)(2,1)S(1)} %all-to-all-done.a, bf16[16,128,1024]{2,1,0:T(8,128)(2,1)S(1)} %copy-done.1), custom_call_target="tpu_custom_call" | custom-call | flops 2000000000 | bytes 6000000 | tf_op jit(solution)/shard_map/product/pallas_call | solution.py:202
  67.6 4.1 %all-to-all-start.1 = ((s16[4,136,1024]{2,1,0:T(8,128)(2,1)}), s16[4,136,1024]{2,1,0:T(8,128)(2,1)S(1)}, u32[]{:S(2)}, u32[]{:S(2)}) async-start(s16[4,136,1024]{2,1,0:T(8,128)(2,1)} %product.1), calls=%async_computation.1 | async-start | bytes 2228224 | tf_op jit(solution)/shard_map/all_to_all | solution.py:216
  71.8 0.0 copy-done.6
  71.8 0.1 broadcast_in_dim.3
  71.8 0.1 reshape.15.keep
  71.9 15.1 %all-to-all-done.1.parts = s16[4,136,1024]{2,1,0:T(8,128)(2,1)S(1)} async-done(((s16[4,136,1024]{2,1,0:T(8,128)(2,1)}), s16[4,136,1024]{2,1,0:T(8,128)(2,1)S(1)}, u32[]{:S(2)}, u32[]{:S(2)}) %all-to-all-start.1) | async-done | bytes 1114144 | tf_op jit(solution)/shard_map/all_to_all | solution.py:216
  87.0 1.1 %filter.1 = f32[128,1024]{1,0:T(8,128)} custom-call(s16[4,136,1024]{2,1,0:T(8,128)(2,1)S(1)} %all-to-all-done.1.parts, f32[2,1024]{1,0:T(2,128)S(1)} %reshape.15.keep), custom_call_target="tpu_custom_call" | custom-call | flops 1000000 | bytes 2000000 | tf_op jit(solution)/shard_map/filter/pallas_call | solution.py:217
  (5 shorter events, 0.0 us)
Async XLA Ops:
  0.0 22.6 %copy-start.2 = (bf16[2,64,1024]{2,1,0:T(8,128)(2,1)S(1)}, bf16[2,64,1024]{2,1,0:T(8,128)(2,1)}, u32[]{:S(2)}) copy-start(bf16[2,64,1024]{2,1,0:T(8,128)(2,1)} %b.1) | copy-start | bytes 786436
  0.0 0.9 %copy-start.3 = (bf16[2,512,64]{1,2,0:T(8,128)(2,1)S(1)}, bf16[2,512,64]{1,2,0:T(8,128)(2,1)}, u32[]{:S(2)}) copy-start(bf16[2,512,64]{1,2,0:T(8,128)(2,1)} %param.5) | copy-start | bytes 393220
  1.0 0.7 copy-start.4
  1.6 21.0 %copy-start.5 = (s32[2,1,16]{2,1,0:T(1,128)S(1)}, s32[2,1,16]{2,1,0:T(1,128)}, u32[]{:S(2)}) copy-start(s32[2,1,16]{2,1,0:T(1,128)} %param.8) | copy-start | bytes 388
  3.2 57.2 %all-to-all-start = ((bf16[16,136,128]{2,1,0:T(8,128)(2,1)}), bf16[16,136,128]{2,1,0:T(8,128)(2,1)S(1)}, u32[]{:S(2)}, u32[]{:S(2)}) async-start(bf16[16,136,128]{2,1,0:T(8,128)(2,1)} %pack_a.1), calls=%async_computation | async-start | bytes 1114112 | tf_op jit(solution)/shard_map/all_to_all | solution.py:178
  45.9 8.9 %collective-permute-start = (bf16[8,136,256]{2,1,0:T(8,128)(2,1)S(1)}, bf16[8,136,256]{2,1,0:T(8,128)(2,1)S(1)}, u32[]{:S(2)}, u32[]{:S(2)}) collective-permute-start(bf16[8,136,256]{2,1,0:T(8,128)(2,1)S(1)} %bitcast.5), channel_id=1, source_target_pairs={{0,64},{64,0},{128,192},{192,128},{256,320},{320,256},{384,448},{4... | collective-permute-start | bytes 1671176 | tf_op jit(solution)/shard_map/ppermute | solution.py:190
  58.4 2.0 %copy-start = (bf16[16,128,1024]{2,1,0:T(8,128)(2,1)}, bf16[16,128,1024]{2,1,0:T(8,128)(2,1)S(1)}, u32[]{:S(2)}) copy-start(bf16[16,128,1024]{2,1,0:T(8,128)(2,1)S(1)} %spread_b.1.b) | copy-start | bytes 12582916
  60.3 2.2 %copy-start.1 = (bf16[16,128,1024]{2,1,0:T(8,128)(2,1)S(1)}, bf16[16,128,1024]{2,1,0:T(8,128)(2,1)}, u32[]{:S(2)}) copy-start(bf16[16,128,1024]{2,1,0:T(8,128)(2,1)} %copy-done) | copy-start | bytes 12582916
  67.6 4.1 %copy-start.6 = (s32[2,16]{1,0:T(2,128)S(1)}, s32[2,16]{1,0:T(2,128)}, u32[]{:S(2)}) copy-start(s32[2,16]{1,0:T(2,128)} %param.9) | copy-start | bytes 388
  67.6 19.4 %all-to-all-start.1 = ((s16[4,136,1024]{2,1,0:T(8,128)(2,1)}), s16[4,136,1024]{2,1,0:T(8,128)(2,1)S(1)}, u32[]{:S(2)}, u32[]{:S(2)}) async-start(s16[4,136,1024]{2,1,0:T(8,128)(2,1)} %product.1), calls=%async_computation.1 | async-start | bytes 2228224 | tf_op jit(solution)/shard_map/all_to_all | solution.py:216

commit v2 on v1

v2 whole, which is shorter than its diff:
```python
import functools

import jax
import jax.numpy as jnp
from jax import lax
from jax.experimental import pallas as pl
from jax.experimental.pallas import tpu as pltpu
from jax.sharding import PartitionSpec as P

BS = 64
BR = 8
BC = 16
KB = 16
MOSTA = 2
MOSTB = 4
STEPS = 2
LAYERS = 4
NONE = 100
EXTRA = 8

F32, BF16, I32, I16 = jnp.float32, jnp.bfloat16, jnp.int32, jnp.int16
ANY = pl.BlockSpec(memory_space=pl.ANY)
VMEM = pl.BlockSpec(memory_space=pltpu.VMEM)


def grant(mib):
    return pltpu.CompilerParams(vmem_limit_bytes=mib * 2**20)


def lanes(rows=1):
    return lax.broadcasted_iota(I32, (rows, 128), 1)


def halves(left, right, rows=1):
    return jnp.where(lanes(rows) < BS, left, right)


def slot_ids(bits, most):
    ids = [jnp.int32(NONE)] * most
    seen = jnp.int32(0)
    for i, bit in enumerate(bits):
        one = bit != 0
        for s in range(most):
            ids[s] = jnp.where(one & (seen == s), jnp.int32(i), ids[s])
        seen = seen + one.astype(I32)
    return ids


def swap_halves(x):
    return pltpu.roll(x, BS, 1)


def compact(panel, pairs, ids):
    outs = [jnp.zeros((BS, 128), F32) for _ in range(len(ids) // 2)]
    for p in range(pairs):
        straight = panel(p)
        turned = swap_halves(straight)
        for o in range(len(outs)):
            want = halves(ids[2 * o], ids[2 * o + 1], BS)
            outs[o] = jnp.where(want == halves(2 * p, 2 * p + 1, BS), straight, outs[o])
            outs[o] = jnp.where(want == halves(2 * p + 1, 2 * p, BS), turned, outs[o])
    return outs


def pack_kernel(a_mask, b_mask, at, b, a_out, b_out, a_bits, b_bits, a_in, b_in, a_packed, b_packed, sems):
    loads = [
        pltpu.make_async_copy(source, target, sems.at[n])
        for n, (source, target) in enumerate(((b_mask, b_bits), (b, b_in), (a_mask, a_bits), (at, a_in)))
    ]
    for load in loads:
        load.start()
    row = lax.broadcasted_iota(I32, (EXTRA, 128), 0)

    loads[0].wait()
    ids = [slot_ids([b_bits[s, j] for j in range(BC)], MOSTB) for s in range(STEPS)]
    loads[1].wait()
    for s in range(STEPS):
        pair = compact(lambda p: b_in[s, :, 128 * p : 128 * p + 128].astype(F32), BC // 2, ids[s])
        for o in range(2):
            b_packed[BS * s : BS * s + BS, 128 * o : 128 * o + 128] = pair[o].astype(BF16)
    for o in range(2):
        index = jnp.where(
            row == 0,
            halves(ids[0][2 * o], ids[0][2 * o + 1], EXTRA),
            halves(ids[1][2 * o], ids[1][2 * o + 1], EXTRA),
        )
        b_packed[128 : 128 + EXTRA, 128 * o : 128 * o + 128] = index.astype(F32).astype(BF16)
    stores = [pltpu.make_async_copy(b_packed, b_out.at[d], sems.at[5 + d]) for d in range(KB)]
    for store in stores:
        store.start()

    loads[2].wait()
    ids = [slot_ids([a_bits[s, i] for i in range(BR)], MOSTA) for s in range(STEPS)]
    loads[3].wait()
    steps = [
        compact(lambda p: a_in[s, :, 128 * p : 128 * p + 128].astype(F32), BR // 2, ids[s])[0]
        for s in range(STEPS)
    ]
    a_packed[0:128, :] = jnp.concatenate(steps, axis=0).T.astype(BF16)
    index = jnp.where(
        row == 0,
        halves(ids[0][0], ids[1][0], EXTRA),
        halves(ids[0][1], ids[1][1], EXTRA),
    )
    a_packed[128 : 128 + EXTRA, :] = index.astype(F32).astype(BF16)
    stores.append(pltpu.make_async_copy(a_packed, a_out, sems.at[4]))
    stores[-1].start()
    for store in stores:
        store.wait()


def spread_b(source, k, row, total):
    for s in range(STEPS):
        parts = []
        for o in range(2):
            index = source[k, 128 : 128 + EXTRA, 128 * o : 128 * o + 128].astype(F32)
            half = source[k, BS * s : BS * s + BS, 128 * o : 128 * o + 128]
            for ids, values in (
                (index, half),
                (swap_halves(index), swap_halves(half.astype(F32)).astype(BF16)),
            ):
                ids = jnp.broadcast_to(ids[s : s + 1], (BS, 128)).astype(BF16)
                parts.append((ids, values))
        for p in range(BC // 2):
            target = halves(2 * p, 2 * p + 1, BS).astype(F32).astype(BF16)
            dense = jnp.zeros((BS, 128), BF16)
            for ids, values in parts:
                dense = jnp.where(ids == target, values, dense)
            total[p // 2, pl.ds(row + BS * s, BS), 128 * (p % 2) : 128 * (p % 2) + 128] = dense


def product_kernel(a, b, out, left, right):
    def spread(k, carry):
        spread_b(b, k, pl.multiple_of(k * 128, 128), right)
        return carry

    lax.fori_loop(0, KB, spread, 0, unroll=2)
    for c in range(KB):
        index = a[c, 128 : 128 + EXTRA, :].astype(F32)
        ids = [jnp.broadcast_to(index[s : s + 1], (BS, 128)).astype(BF16) for s in range(MOSTA)]
        for i in range(BR):
            dense = jnp.zeros((BS, 128), BF16)
            for s in range(MOSTA):
                dense = jnp.where(ids[s] == jnp.bfloat16(i), a[c, BS * s : BS * s + BS, :], dense)
            left[BS * i : BS * i + BS, 128 * c : 128 * c + 128] = dense
    rows = out.shape[1] - EXTRA
    tiles, _, width = right.shape
    for t in range(tiles):
        cols = slice(width * t, width * t + width)
        total = jnp.dot(left[...], right[t], preferred_element_type=F32)
        for l in range(LAYERS):
            part = total[rows * l : rows * l + rows]
            top = jnp.max(jnp.abs(part), axis=0, keepdims=True)
            power = jnp.floor(jnp.log2(jnp.maximum(top, 1e-30))) - 13.0
            out[l, 0:rows, cols] = jnp.round(part * jnp.exp2(-power)).astype(I32).astype(I16)
            power = jnp.broadcast_to(power, (EXTRA, width))
            out[l, rows : rows + EXTRA, cols] = power.astype(I32).astype(I16)


def filter_kernel(parts, keep, out):
    rows = out.shape[0]
    total = None
    for l in range(LAYERS):
        power = parts[l, rows : rows + EXTRA, :].astype(I32).astype(F32)[0:1]
        term = parts[l, 0:rows, :].astype(I32).astype(F32) * jnp.exp2(power)
        total = term if total is None else total + term
    for i in range(rows // BS):
        out[BS * i : BS * i + BS, :] = total[BS * i : BS * i + BS] * keep[i : i + 1, :]


def body(a_panel, b_panel, a_mask, b_mask, c_pattern):
    rows = 128 + EXTRA
    a_sent, b_sent = pl.pallas_call(
        pack_kernel,
        out_shape=(
            jax.ShapeDtypeStruct((rows, 128), BF16),
            jax.ShapeDtypeStruct((KB, rows, 256), BF16),
        ),
        in_specs=[ANY] * 4,
        out_specs=(ANY, ANY),
        scratch_shapes=[
            pltpu.SMEM((STEPS, BR), I32),
            pltpu.SMEM((STEPS, BC), I32),
            pltpu.VMEM((STEPS, BS, BR * BS), BF16),
            pltpu.VMEM((STEPS, BS, BC * BS), BF16),
            pltpu.VMEM((rows, 128), BF16),
            pltpu.VMEM((rows, 256), BF16),
            pltpu.SemaphoreType.DMA((5 + KB,)),
        ],
        cost_estimate=pl.CostEstimate(flops=10**6, bytes_accessed=2 * 10**6, transcendentals=0),
        name="pack",
    )(
        a_mask.reshape(STEPS, BR),
        b_mask.reshape(STEPS, BC),
        jnp.swapaxes(a_panel, 1, 2),
        b_panel,
    )
    b_all = lax.all_to_all(b_sent, "row", 0, 0, tiled=True)
    a_all = lax.all_gather(a_sent, "col")
    keep = jnp.repeat(c_pattern.astype(F32), BS, axis=1)
    sums = pl.pallas_call(
        product_kernel,
        out_shape=jax.ShapeDtypeStruct((LAYERS, 128 + EXTRA, 1024), I16),
        in_specs=[VMEM, VMEM],
        out_specs=VMEM,
        scratch_shapes=[
            pltpu.VMEM((BR * BS, KB * 128), BF16),
            pltpu.VMEM((4, KB * 128, 256), BF16),
        ],
        cost_estimate=pl.CostEstimate(flops=2 * 10**9, bytes_accessed=6 * 10**6, transcendentals=0),
        compiler_params=grant(24),
        name="product",
    )(a_all, b_all)
    parts = lax.all_to_all(sums, "layer", 0, 0, tiled=True)
    return pl.pallas_call(
        filter_kernel,
        out_shape=jax.ShapeDtypeStruct((128, 1024), F32),
        in_specs=[VMEM, VMEM],
        out_specs=VMEM,
        cost_estimate=pl.CostEstimate(flops=10**6, bytes_accessed=2 * 10**6, transcendentals=0),
        compiler_params=grant(8),
        name="filter",
    )(parts, keep)


def solution(mesh):
    spec = P("layer", "row", "col")
    out = P(("row", "layer"), "col")
    return jax.shard_map(
        body, mesh=mesh, in_specs=(spec, spec, spec, spec, out), out_specs=out, check_vma=False
    )
```

time: 88.5 us -> 77.7 us (0.88)
  the two profiles are of different devices: /device:TPU:1 before, /device:TPU:8 now
where the time goes in v2:
time: 77.7 us; the launch traced here: 77.4 us
  blocking collectives  36.5 us (47%)
  starting transfers between devices  21 us (27%)
  waiting for transfers between devices  11.1 us (14%)
  Pallas kernels  8.6 us (11%)
    all_gather x1, blocking collectives, body(): a_all = lax.all_gather(a_sent, 'col')  36.5 us
    all_to_all x1, starting transfers between devices, body(): b_all = lax.all_to_all(b_sent, 'row', 0, 0, tiled=True)  16.6 us
    all_to_all x1, waiting for transfers between devices, body(): parts = lax.all_to_all(sums, 'layer', 0, 0, tiled=True)  11.1 us
    pallas_call x1, Pallas kernels, body(): pl.pallas_call(product_kernel, out_shape=jax.ShapeDtypeStruct((LAYERS, 12...  5.21 us
    all_to_all x1, starting transfers between devices, body(): parts = lax.all_to_all(sums, 'layer', 0, 0, tiled=True)  4.42 us
    pallas_call x1, Pallas kernels, body(): pl.pallas_call(pack_kernel, out_shape=(jax.ShapeDtypeStruct((rows, 128),...  2.31 us
  transfers between devices with their start and end apart: 2, of which 1 were waited for; matrix products, arithmetic and copies ran while one was open for 0% of the time, Pallas kernels for 0%

profile of v2, /device:TPU:8, one launch (start us, length us, event | category | flops | bytes accessed | tf_op | source)
XLA Modules:
  0.0 77.4 jit_solution(14932759498194668822)
XLA Ops:
  0.0 2.3 %pack.1 = (bf16[136,128]{1,0:T(8,128)(2,1)}, bf16[16,136,256]{2,1,0:T(8,128)(2,1)}) custom-call(s32[2,8]{1,0:T(2,128)} %bitcast.6, s32[2,16]{1,0:T(2,128)} %bitcast.7, bf16[2,64,512]{2,1,0:T(8,128)(2,1)} %bitcast.5, bf16[2,64,1024]{2,1,0:T(8,128)(2,1)} %b.1), custom_call_target="tpu_custom_call" | custom-call | flops 1000000 | bytes 2000000 | tf_op jit(solution)/shard_map/pack/pallas_call | solution.py:173
  2.3 0.0 copy-start
  2.3 16.6 %all-to-all-start = ((bf16[16,136,256]{2,1,0:T(8,128)(2,1)}), bf16[16,136,256]{2,1,0:T(8,128)(2,1)S(1)}, u32[]{:S(2)}, u32[]{:S(2)}) async-start(bf16[16,136,256]{2,1,0:T(8,128)(2,1)} %get-tuple-element.8), calls=%async_computation | async-start | bytes 2228224 | tf_op jit(solution)/shard_map/all_to_all | solution.py:198
  18.9 0.0 copy-done
  18.9 36.5 %all-gather = bf16[2176,128]{1,0:T(8,128)(2,1)S(1)} all-gather(bf16[136,128]{1,0:T(8,128)(2,1)S(1)} %copy-done), channel_id=2, replica_groups=mesh['row'=16,'col'=16,'layer'=4] {'col'}, dimensions={0}, use_global_device_ids=true | all-gather | bytes 591872 | tf_op jit(solution)/shard_map/all_gather | solution.py:199
  55.4 0.0 all-to-all-done.b
  55.4 5.2 %product.1 = s16[4,136,1024]{2,1,0:T(8,128)(2,1)} custom-call(bf16[16,136,128]{2,1,0:T(8,128)(2,1)S(1)} %bitcast.4, bf16[16,136,256]{2,1,0:T(8,128)(2,1)S(1)} %all-to-all-done.b), custom_call_target="tpu_custom_call" | custom-call | flops 2000000000 | bytes 6000000 | tf_op jit(solution)/shard_map/product/pallas_call | solution.py:201
  60.6 0.0 copy-start.1
  60.6 4.4 %all-to-all-start.1 = ((s16[4,136,1024]{2,1,0:T(8,128)(2,1)}), s16[4,136,1024]{2,1,0:T(8,128)(2,1)S(1)}, u32[]{:S(2)}, u32[]{:S(2)}) async-start(s16[4,136,1024]{2,1,0:T(8,128)(2,1)} %product.1), calls=%async_computation.1 | async-start | bytes 2228224 | tf_op jit(solution)/shard_map/all_to_all | solution.py:214
  65.0 0.0 copy-done.1
  65.0 0.1 broadcast_in_dim.3
  65.1 0.1 reshape.11.keep
  65.2 11.1 %all-to-all-done.1.parts = s16[4,136,1024]{2,1,0:T(8,128)(2,1)S(1)} async-done(((s16[4,136,1024]{2,1,0:T(8,128)(2,1)}), s16[4,136,1024]{2,1,0:T(8,128)(2,1)S(1)}, u32[]{:S(2)}, u32[]{:S(2)}) %all-to-all-start.1) | async-done | bytes 1114144 | tf_op jit(solution)/shard_map/all_to_all | solution.py:214
  76.3 1.1 %filter.1 = f32[128,1024]{1,0:T(8,128)} custom-call(s16[4,136,1024]{2,1,0:T(8,128)(2,1)S(1)} %all-to-all-done.1.parts, f32[2,1024]{1,0:T(2,128)S(1)} %reshape.11.keep), custom_call_target="tpu_custom_call" | custom-call | flops 1000000 | bytes 2000000 | tf_op jit(solution)/shard_map/filter/pallas_call | solution.py:215
  (1 shorter events, 0.0 us)
Async XLA Ops:
  2.3 16.6 %copy-start = (bf16[136,128]{1,0:T(8,128)(2,1)S(1)}, bf16[136,128]{1,0:T(8,128)(2,1)}, u32[]{:S(2)}) copy-start(bf16[136,128]{1,0:T(8,128)(2,1)} %get-tuple-element.7) | copy-start | bytes 104452
  2.3 53.1 %all-to-all-start = ((bf16[16,136,256]{2,1,0:T(8,128)(2,1)}), bf16[16,136,256]{2,1,0:T(8,128)(2,1)S(1)}, u32[]{:S(2)}, u32[]{:S(2)}) async-start(bf16[16,136,256]{2,1,0:T(8,128)(2,1)} %get-tuple-element.8), calls=%async_computation | async-start | bytes 2228224 | tf_op jit(solution)/shard_map/all_to_all | solution.py:198
  60.6 4.4 %copy-start.1 = (s32[2,16]{1,0:T(2,128)S(1)}, s32[2,16]{1,0:T(2,128)}, u32[]{:S(2)}) copy-start(s32[2,16]{1,0:T(2,128)} %param.9) | copy-start | bytes 388
  60.6 15.7 %all-to-all-start.1 = ((s16[4,136,1024]{2,1,0:T(8,128)(2,1)}), s16[4,136,1024]{2,1,0:T(8,128)(2,1)S(1)}, u32[]{:S(2)}, u32[]{:S(2)}) async-start(s16[4,136,1024]{2,1,0:T(8,128)(2,1)} %product.1), calls=%async_computation.1 | async-start | bytes 2228224 | tf_op jit(solution)/shard_map/all_to_all | solution.py:214

commit v3 on v2

--- a/solution.py
+++ b/solution.py
@@ -109,32 +109,28 @@
         store.wait()
 
 
-def spread_b(source, k, row, total):
-    for s in range(STEPS):
-        parts = []
-        for o in range(2):
-            index = source[k, 128 : 128 + EXTRA, 128 * o : 128 * o + 128].astype(F32)
-            half = source[k, BS * s : BS * s + BS, 128 * o : 128 * o + 128]
-            for ids, values in (
-                (index, half),
-                (swap_halves(index), swap_halves(half.astype(F32)).astype(BF16)),
-            ):
-                ids = jnp.broadcast_to(ids[s : s + 1], (BS, 128)).astype(BF16)
-                parts.append((ids, values))
-        for p in range(BC // 2):
-            target = halves(2 * p, 2 * p + 1, BS).astype(F32).astype(BF16)
-            dense = jnp.zeros((BS, 128), BF16)
-            for ids, values in parts:
-                dense = jnp.where(ids == target, values, dense)
-            total[p // 2, pl.ds(row + BS * s, BS), 128 * (p % 2) : 128 * (p % 2) + 128] = dense
-
-
-def product_kernel(a, b, out, left, right):
-    def spread(k, carry):
-        spread_b(b, k, pl.multiple_of(k * 128, 128), right)
-        return carry
-
-    lax.fori_loop(0, KB, spread, 0, unroll=2)
+def turn(b, k, s):
+    parts = []
+    for o in range(2):
+        index = b[k, 128 : 128 + EXTRA, 128 * o : 128 * o + 128].astype(F32)
+        half = b[k, BS * s : BS * s + BS, 128 * o : 128 * o + 128]
+        for ids, values in (
+            (index, half),
+            (swap_halves(index), swap_halves(half.astype(F32)).astype(BF16)),
+        ):
+            parts.append((jnp.broadcast_to(ids[s : s + 1], (BS, 128)).astype(BF16), values))
+    return parts
+
+
+def pick(parts, p):
+    target = halves(2 * p, 2 * p + 1, BS).astype(F32).astype(BF16)
+    dense = jnp.zeros((BS, 128), BF16)
+    for ids, values in parts:
+        dense = jnp.where(ids == target, values, dense)
+    return dense
+
+
+def product_kernel(a, b, out, left):
     for c in range(KB):
         index = a[c, 128 : 128 + EXTRA, :].astype(F32)
         ids = [jnp.broadcast_to(index[s : s + 1], (BS, 128)).astype(BF16) for s in range(MOSTA)]
@@ -144,10 +140,15 @@
                 dense = jnp.where(ids[s] == jnp.bfloat16(i), a[c, BS * s : BS * s + BS, :], dense)
             left[BS * i : BS * i + BS, 128 * c : 128 * c + 128] = dense
     rows = out.shape[1] - EXTRA
-    tiles, _, width = right.shape
+    tiles, width = 1, 1024
     for t in range(tiles):
         cols = slice(width * t, width * t + width)
-        total = jnp.dot(left[...], right[t], preferred_element_type=F32)
+        dense = []
+        for k in range(KB):
+            for s in range(STEPS):
+                parts = turn(b, k, s)
+                dense.append(jnp.concatenate([pick(parts, h) for h in range(8)], axis=1))
+        total = jnp.dot(left[...], jnp.concatenate(dense, axis=0), preferred_element_type=F32)
         for l in range(LAYERS):
             part = total[rows * l : rows * l + rows]
             top = jnp.max(jnp.abs(part), axis=0, keepdims=True)
@@ -205,7 +206,6 @@
         out_specs=VMEM,
         scratch_shapes=[
             pltpu.VMEM((BR * BS, KB * 128), BF16),
-            pltpu.VMEM((4, KB * 128, 256), BF16),
         ],
         cost_estimate=pl.CostEstimate(flops=2 * 10**9, bytes_accessed=6 * 10**6, transcendentals=0),
         compiler_params=grant(24),

time: 77.7 us -> 76.3 us (0.982)
  Pallas kernels: 8.6 us -> 7.21 us
    pallas_call x1, Pallas kernels: 5.21 us -> 3.82 us  [body(): pl.pallas_call(product_kernel, out_shape=jax.ShapeDtypeStruct((LAYERS, 12...]
where the time goes in v3:
time: 76.3 us; the launch traced here: 76 us
  blocking collectives  36.5 us (48%)
  starting transfers between devices  21 us (28%)
  waiting for transfers between devices  11.1 us (15%)
  Pallas kernels  7.21 us (9%)
    all_gather x1, blocking collectives, body(): a_all = lax.all_gather(a_sent, 'col')  36.5 us
    all_to_all x1, starting transfers between devices, body(): b_all = lax.all_to_all(b_sent, 'row', 0, 0, tiled=True)  16.6 us
    all_to_all x1, waiting for transfers between devices, body(): parts = lax.all_to_all(sums, 'layer', 0, 0, tiled=True)  11.1 us
    all_to_all x1, starting transfers between devices, body(): parts = lax.all_to_all(sums, 'layer', 0, 0, tiled=True)  4.42 us
    pallas_call x1, Pallas kernels, body(): pl.pallas_call(product_kernel, out_shape=jax.ShapeDtypeStruct((LAYERS, 12...  3.82 us
    pallas_call x1, Pallas kernels, body(): pl.pallas_call(pack_kernel, out_shape=(jax.ShapeDtypeStruct((rows, 128),...  2.31 us
  transfers between devices with their start and end apart: 2, of which 1 were waited for; matrix products, arithmetic and copies ran while one was open for 0% of the time, Pallas kernels for 0%

profile of v3, /device:TPU:8, one launch (start us, length us, event | category | flops | bytes accessed | tf_op | source)
XLA Modules:
  0.0 76.0 jit_solution(1070780667214392505)
XLA Ops:
  0.0 2.3 %pack.1 = (bf16[136,128]{1,0:T(8,128)(2,1)}, bf16[16,136,256]{2,1,0:T(8,128)(2,1)}) custom-call(s32[2,8]{1,0:T(2,128)} %bitcast.6, s32[2,16]{1,0:T(2,128)} %bitcast.7, bf16[2,64,512]{2,1,0:T(8,128)(2,1)} %bitcast.5, bf16[2,64,1024]{2,1,0:T(8,128)(2,1)} %b.1), custom_call_target="tpu_custom_call" | custom-call | flops 1000000 | bytes 2000000 | tf_op jit(solution)/shard_map/pack/pallas_call | solution.py:174
  2.3 0.0 copy-start
  2.3 16.6 %all-to-all-start = ((bf16[16,136,256]{2,1,0:T(8,128)(2,1)}), bf16[16,136,256]{2,1,0:T(8,128)(2,1)S(1)}, u32[]{:S(2)}, u32[]{:S(2)}) async-start(bf16[16,136,256]{2,1,0:T(8,128)(2,1)} %get-tuple-element.8), calls=%async_computation | async-start | bytes 2228224 | tf_op jit(solution)/shard_map/all_to_all | solution.py:199
  18.9 0.0 copy-done
  18.9 36.5 %all-gather = bf16[2176,128]{1,0:T(8,128)(2,1)S(1)} all-gather(bf16[136,128]{1,0:T(8,128)(2,1)S(1)} %copy-done), channel_id=2, replica_groups=mesh['row'=16,'col'=16,'layer'=4] {'col'}, dimensions={0}, use_global_device_ids=true | all-gather | bytes 591872 | tf_op jit(solution)/shard_map/all_gather | solution.py:200
  55.4 0.0 all-to-all-done.b
  55.4 3.8 %product.1 = s16[4,136,1024]{2,1,0:T(8,128)(2,1)} custom-call(bf16[16,136,128]{2,1,0:T(8,128)(2,1)S(1)} %bitcast.4, bf16[16,136,256]{2,1,0:T(8,128)(2,1)S(1)} %all-to-all-done.b), custom_call_target="tpu_custom_call" | custom-call | flops 2000000000 | bytes 6000000 | tf_op jit(solution)/shard_map/product/pallas_call | solution.py:202
  59.2 0.0 copy-start.1
  59.2 4.4 %all-to-all-start.1 = ((s16[4,136,1024]{2,1,0:T(8,128)(2,1)}), s16[4,136,1024]{2,1,0:T(8,128)(2,1)S(1)}, u32[]{:S(2)}, u32[]{:S(2)}) async-start(s16[4,136,1024]{2,1,0:T(8,128)(2,1)} %product.1), calls=%async_computation.1 | async-start | bytes 2228224 | tf_op jit(solution)/shard_map/all_to_all | solution.py:214
  63.6 0.0 copy-done.1
  63.6 0.1 broadcast_in_dim.3
  63.7 0.1 reshape.11.keep
  63.8 11.1 %all-to-all-done.1.parts = s16[4,136,1024]{2,1,0:T(8,128)(2,1)S(1)} async-done(((s16[4,136,1024]{2,1,0:T(8,128)(2,1)}), s16[4,136,1024]{2,1,0:T(8,128)(2,1)S(1)}, u32[]{:S(2)}, u32[]{:S(2)}) %all-to-all-start.1) | async-done | bytes 1114144 | tf_op jit(solution)/shard_map/all_to_all | solution.py:214
  74.9 1.1 %filter.1 = f32[128,1024]{1,0:T(8,128)} custom-call(s16[4,136,1024]{2,1,0:T(8,128)(2,1)S(1)} %all-to-all-done.1.parts, f32[2,1024]{1,0:T(2,128)S(1)} %reshape.11.keep), custom_call_target="tpu_custom_call" | custom-call | flops 1000000 | bytes 2000000 | tf_op jit(solution)/shard_map/filter/pallas_call | solution.py:215
  (1 shorter events, 0.0 us)
Async XLA Ops:
  2.3 16.6 %copy-start = (bf16[136,128]{1,0:T(8,128)(2,1)S(1)}, bf16[136,128]{1,0:T(8,128)(2,1)}, u32[]{:S(2)}) copy-start(bf16[136,128]{1,0:T(8,128)(2,1)} %get-tuple-element.7) | copy-start | bytes 104452
  2.3 53.1 %all-to-all-start = ((bf16[16,136,256]{2,1,0:T(8,128)(2,1)}), bf16[16,136,256]{2,1,0:T(8,128)(2,1)S(1)}, u32[]{:S(2)}, u32[]{:S(2)}) async-start(bf16[16,136,256]{2,1,0:T(8,128)(2,1)} %get-tuple-element.8), calls=%async_computation | async-start | bytes 2228224 | tf_op jit(solution)/shard_map/all_to_all | solution.py:199
  59.2 4.4 %copy-start.1 = (s32[2,16]{1,0:T(2,128)S(1)}, s32[2,16]{1,0:T(2,128)}, u32[]{:S(2)}) copy-start(s32[2,16]{1,0:T(2,128)} %param.9) | copy-start | bytes 388
  59.2 15.7 %all-to-all-start.1 = ((s16[4,136,1024]{2,1,0:T(8,128)(2,1)}), s16[4,136,1024]{2,1,0:T(8,128)(2,1)S(1)}, u32[]{:S(2)}, u32[]{:S(2)}) async-start(s16[4,136,1024]{2,1,0:T(8,128)(2,1)} %product.1), calls=%async_computation.1 | async-start | bytes 2228224 | tf_op jit(solution)/shard_map/all_to_all | solution.py:214

commit v4 on v3

--- a/solution.py
+++ b/solution.py
@@ -16,6 +16,7 @@
 STEPS = 2
 LAYERS = 4
 NONE = 100
+PIECE = 32
 EXTRA = 8
 
 F32, BF16, I32, I16 = jnp.float32, jnp.bfloat16, jnp.int32, jnp.int16
@@ -47,18 +48,23 @@
 
 
 def swap_halves(x):
-    return pltpu.roll(x, BS, 1)
+    return jnp.concatenate([x[:, BS:], x[:, :BS]], axis=1)
+
+
+def narrow(ids):
+    return ids.astype(F32).astype(BF16)
 
 
 def compact(panel, pairs, ids):
-    outs = [jnp.zeros((BS, 128), F32) for _ in range(len(ids) // 2)]
+    outs = [jnp.zeros((BS, 128), BF16) for _ in range(len(ids) // 2)]
+    wants = [narrow(halves(ids[2 * o], ids[2 * o + 1], BS)) for o in range(len(outs))]
     for p in range(pairs):
         straight = panel(p)
         turned = swap_halves(straight)
+        here, there = (narrow(halves(*at, BS)) for at in ((2 * p, 2 * p + 1), (2 * p + 1, 2 * p)))
         for o in range(len(outs)):
-            want = halves(ids[2 * o], ids[2 * o + 1], BS)
-            outs[o] = jnp.where(want == halves(2 * p, 2 * p + 1, BS), straight, outs[o])
-            outs[o] = jnp.where(want == halves(2 * p + 1, 2 * p, BS), turned, outs[o])
+            outs[o] = jnp.where(wants[o] == here, straight, outs[o])
+            outs[o] = jnp.where(wants[o] == there, turned, outs[o])
     return outs
 
 
@@ -75,16 +81,16 @@
     ids = [slot_ids([b_bits[s, j] for j in range(BC)], MOSTB) for s in range(STEPS)]
     loads[1].wait()
     for s in range(STEPS):
-        pair = compact(lambda p: b_in[s, :, 128 * p : 128 * p + 128].astype(F32), BC // 2, ids[s])
+        pair = compact(lambda p: b_in[s, :, 128 * p : 128 * p + 128], BC // 2, ids[s])
         for o in range(2):
-            b_packed[BS * s : BS * s + BS, 128 * o : 128 * o + 128] = pair[o].astype(BF16)
+            b_packed[BS * s : BS * s + BS, 128 * o : 128 * o + 128] = pair[o]
     for o in range(2):
         index = jnp.where(
             row == 0,
             halves(ids[0][2 * o], ids[0][2 * o + 1], EXTRA),
             halves(ids[1][2 * o], ids[1][2 * o + 1], EXTRA),
         )
-        b_packed[128 : 128 + EXTRA, 128 * o : 128 * o + 128] = index.astype(F32).astype(BF16)
+        b_packed[128 : 128 + EXTRA, 128 * o : 128 * o + 128] = narrow(index)
     stores = [pltpu.make_async_copy(b_packed, b_out.at[d], sems.at[5 + d]) for d in range(KB)]
     for store in stores:
         store.start()
@@ -93,16 +99,16 @@
     ids = [slot_ids([a_bits[s, i] for i in range(BR)], MOSTA) for s in range(STEPS)]
     loads[3].wait()
     steps = [
-        compact(lambda p: a_in[s, :, 128 * p : 128 * p + 128].astype(F32), BR // 2, ids[s])[0]
+        compact(lambda p: a_in[s, :, 128 * p : 128 * p + 128], BR // 2, ids[s])[0]
         for s in range(STEPS)
     ]
-    a_packed[0:128, :] = jnp.concatenate(steps, axis=0).T.astype(BF16)
+    a_packed[0:128, :] = jnp.concatenate(steps, axis=0).astype(F32).T.astype(BF16)
     index = jnp.where(
         row == 0,
         halves(ids[0][0], ids[1][0], EXTRA),
         halves(ids[0][1], ids[1][1], EXTRA),
     )
-    a_packed[128 : 128 + EXTRA, :] = index.astype(F32).astype(BF16)
+    a_packed[128 : 128 + EXTRA, :] = narrow(index)
     stores.append(pltpu.make_async_copy(a_packed, a_out, sems.at[4]))
     stores[-1].start()
     for store in stores:
@@ -116,7 +122,7 @@
         half = b[k, BS * s : BS * s + BS, 128 * o : 128 * o + 128]
         for ids, values in (
             (index, half),
-            (swap_halves(index), swap_halves(half.astype(F32)).astype(BF16)),
+            (swap_halves(index), jnp.concatenate([half[:, BS:], half[:, :BS]], axis=1)),
         ):
             parts.append((jnp.broadcast_to(ids[s : s + 1], (BS, 128)).astype(BF16), values))
     return parts
@@ -130,25 +136,30 @@
     return dense
 
 
-def product_kernel(a, b, out, left):
+def product_kernel(a, b, out):
+    columns = []
     for c in range(KB):
         index = a[c, 128 : 128 + EXTRA, :].astype(F32)
         ids = [jnp.broadcast_to(index[s : s + 1], (BS, 128)).astype(BF16) for s in range(MOSTA)]
+        blocks = []
         for i in range(BR):
             dense = jnp.zeros((BS, 128), BF16)
             for s in range(MOSTA):
                 dense = jnp.where(ids[s] == jnp.bfloat16(i), a[c, BS * s : BS * s + BS, :], dense)
-            left[BS * i : BS * i + BS, 128 * c : 128 * c + 128] = dense
+            blocks.append(dense)
+        columns.append(jnp.concatenate(blocks, axis=0))
+    left = jnp.concatenate(columns, axis=1)
+    turned = {(k, s): turn(b, k, s) for k in range(KB) for s in range(STEPS)}
     rows = out.shape[1] - EXTRA
-    tiles, width = 1, 1024
+    tiles, width = 2, 512
     for t in range(tiles):
         cols = slice(width * t, width * t + width)
         dense = []
         for k in range(KB):
             for s in range(STEPS):
-                parts = turn(b, k, s)
-                dense.append(jnp.concatenate([pick(parts, h) for h in range(8)], axis=1))
-        total = jnp.dot(left[...], jnp.concatenate(dense, axis=0), preferred_element_type=F32)
+                parts = turned[k, s]
+                dense.append(jnp.concatenate([pick(parts, 4 * t + h) for h in range(4)], axis=1))
+        total = jnp.dot(left, jnp.concatenate(dense, axis=0), preferred_element_type=F32)
         for l in range(LAYERS):
             part = total[rows * l : rows * l + rows]
             top = jnp.max(jnp.abs(part), axis=0, keepdims=True)
@@ -158,15 +169,21 @@
             out[l, rows : rows + EXTRA, cols] = power.astype(I32).astype(I16)
 
 
-def filter_kernel(parts, keep, out):
+def filter_kernel(parts, keep, out, total, sems):
     rows = out.shape[0]
-    total = None
-    for l in range(LAYERS):
-        power = parts[l, rows : rows + EXTRA, :].astype(I32).astype(F32)[0:1]
-        term = parts[l, 0:rows, :].astype(I32).astype(F32) * jnp.exp2(power)
-        total = term if total is None else total + term
-    for i in range(rows // BS):
-        out[BS * i : BS * i + BS, :] = total[BS * i : BS * i + BS] * keep[i : i + 1, :]
+    scales = [jnp.exp2(parts[l, rows : rows + EXTRA, :].astype(I32).astype(F32)[0:1]) for l in range(LAYERS)]
+    stores = []
+    for n, r in enumerate(range(0, rows, PIECE)):
+        some = None
+        for l in range(LAYERS):
+            term = parts[l, r : r + PIECE, :].astype(I32).astype(F32) * scales[l]
+            some = term if some is None else some + term
+        total[r : r + PIECE, :] = some * keep[r // BS : r // BS + 1, :]
+        here = pl.ds(r, PIECE)
+        stores.append(pltpu.make_async_copy(total.at[here], out.at[here], sems.at[n]))
+        stores[-1].start()
+    for store in stores:
+        store.wait()
 
 
 def body(a_panel, b_panel, a_mask, b_mask, c_pattern):
@@ -204,9 +221,6 @@
         out_shape=jax.ShapeDtypeStruct((LAYERS, 128 + EXTRA, 1024), I16),
         in_specs=[VMEM, VMEM],
         out_specs=VMEM,
-        scratch_shapes=[
-            pltpu.VMEM((BR * BS, KB * 128), BF16),
-        ],
         cost_estimate=pl.CostEstimate(flops=2 * 10**9, bytes_accessed=6 * 10**6, transcendentals=0),
         compiler_params=grant(24),
         name="product",
@@ -216,7 +230,8 @@
         filter_kernel,
         out_shape=jax.ShapeDtypeStruct((128, 1024), F32),
         in_specs=[VMEM, VMEM],
-        out_specs=VMEM,
+        out_specs=ANY,
+        scratch_shapes=[pltpu.VMEM((128, 1024), F32), pltpu.SemaphoreType.DMA((128 // PIECE,))],
         cost_estimate=pl.CostEstimate(flops=10**6, bytes_accessed=2 * 10**6, transcendentals=0),
         compiler_params=grant(8),
         name="filter",

time: 76.3 us -> 75.9 us (level)
  no operation moved by 1% of the time
where the time goes in v4:
time: 75.9 us; the launch traced here: 75.6 us
  blocking collectives  36.5 us (48%)
  starting transfers between devices  21 us (28%)
  waiting for transfers between devices  11.1 us (15%)
  Pallas kernels  6.85 us (9%)
    all_gather x1, blocking collectives, body(): a_all = lax.all_gather(a_sent, 'col')  36.5 us
    all_to_all x1, starting transfers between devices, body(): b_all = lax.all_to_all(b_sent, 'row', 0, 0, tiled=True)  16.6 us
    all_to_all x1, waiting for transfers between devices, body(): parts = lax.all_to_all(sums, 'layer', 0, 0, tiled=True)  11.1 us
    all_to_all x1, starting transfers between devices, body(): parts = lax.all_to_all(sums, 'layer', 0, 0, tiled=True)  4.42 us
    pallas_call x1, Pallas kernels, body(): pl.pallas_call(product_kernel, out_shape=jax.ShapeDtypeStruct((LAYERS, 12...  3.59 us
    pallas_call x1, Pallas kernels, body(): pl.pallas_call(pack_kernel, out_shape=(jax.ShapeDtypeStruct((rows, 128),...  2.28 us
  transfers between devices with their start and end apart: 2, of which 1 were waited for; matrix products, arithmetic and copies ran while one was open for 0% of the time, Pallas kernels for 0%

profile of v4, /device:TPU:8, one launch (start us, length us, event | category | flops | bytes accessed | tf_op | source)
XLA Modules:
  0.0 75.6 jit_solution(2019790141282550471)
XLA Ops:
  0.0 2.3 %pack.1 = (bf16[136,128]{1,0:T(8,128)(2,1)}, bf16[16,136,256]{2,1,0:T(8,128)(2,1)}) custom-call(s32[2,8]{1,0:T(2,128)} %bitcast.6, s32[2,16]{1,0:T(2,128)} %bitcast.7, bf16[2,64,512]{2,1,0:T(8,128)(2,1)} %bitcast.5, bf16[2,64,1024]{2,1,0:T(8,128)(2,1)} %b.1), custom_call_target="tpu_custom_call" | custom-call | flops 1000000 | bytes 2000000 | tf_op jit(solution)/shard_map/pack/pallas_call | solution.py:191
  2.3 0.0 copy-start
  2.3 16.6 %all-to-all-start = ((bf16[16,136,256]{2,1,0:T(8,128)(2,1)}), bf16[16,136,256]{2,1,0:T(8,128)(2,1)S(1)}, u32[]{:S(2)}, u32[]{:S(2)}) async-start(bf16[16,136,256]{2,1,0:T(8,128)(2,1)} %get-tuple-element.8), calls=%async_computation | async-start | bytes 2228224 | tf_op jit(solution)/shard_map/all_to_all | solution.py:216
  18.9 0.0 copy-done
  18.9 36.5 %all-gather = bf16[2176,128]{1,0:T(8,128)(2,1)S(1)} all-gather(bf16[136,128]{1,0:T(8,128)(2,1)S(1)} %copy-done), channel_id=2, replica_groups=mesh['row'=16,'col'=16,'layer'=4] {'col'}, dimensions={0}, use_global_device_ids=true | all-gather | bytes 591872 | tf_op jit(solution)/shard_map/all_gather | solution.py:217
  55.4 0.0 all-to-all-done.b
  55.4 3.6 %product.1 = s16[4,136,1024]{2,1,0:T(8,128)(2,1)} custom-call(bf16[16,136,128]{2,1,0:T(8,128)(2,1)S(1)} %bitcast.4, bf16[16,136,256]{2,1,0:T(8,128)(2,1)S(1)} %all-to-all-done.b), custom_call_target="tpu_custom_call" | custom-call | flops 2000000000 | bytes 6000000 | tf_op jit(solution)/shard_map/product/pallas_call | solution.py:219
  59.0 0.0 copy-start.1
  59.0 4.4 %all-to-all-start.1 = ((s16[4,136,1024]{2,1,0:T(8,128)(2,1)}), s16[4,136,1024]{2,1,0:T(8,128)(2,1)S(1)}, u32[]{:S(2)}, u32[]{:S(2)}) async-start(s16[4,136,1024]{2,1,0:T(8,128)(2,1)} %product.1), calls=%async_computation.1 | async-start | bytes 2228224 | tf_op jit(solution)/shard_map/all_to_all | solution.py:228
  63.4 0.0 copy-done.1
  63.4 0.1 broadcast_in_dim.3
  63.5 0.1 reshape.11.keep
  63.5 11.1 %all-to-all-done.1.parts = s16[4,136,1024]{2,1,0:T(8,128)(2,1)S(1)} async-done(((s16[4,136,1024]{2,1,0:T(8,128)(2,1)}), s16[4,136,1024]{2,1,0:T(8,128)(2,1)S(1)}, u32[]{:S(2)}, u32[]{:S(2)}) %all-to-all-start.1) | async-done | bytes 1114144 | tf_op jit(solution)/shard_map/all_to_all | solution.py:228
  74.6 1.0 %filter.1 = f32[128,1024]{1,0:T(8,128)} custom-call(s16[4,136,1024]{2,1,0:T(8,128)(2,1)S(1)} %all-to-all-done.1.parts, f32[2,1024]{1,0:T(2,128)S(1)} %reshape.11.keep), custom_call_target="tpu_custom_call" | custom-call | flops 1000000 | bytes 2000000 | tf_op jit(solution)/shard_map/filter/pallas_call | solution.py:229
  (1 shorter events, 0.0 us)
Async XLA Ops:
  2.3 16.6 %copy-start = (bf16[136,128]{1,0:T(8,128)(2,1)S(1)}, bf16[136,128]{1,0:T(8,128)(2,1)}, u32[]{:S(2)}) copy-start(bf16[136,128]{1,0:T(8,128)(2,1)} %get-tuple-element.7) | copy-start | bytes 104452
  2.3 53.1 %all-to-all-start = ((bf16[16,136,256]{2,1,0:T(8,128)(2,1)}), bf16[16,136,256]{2,1,0:T(8,128)(2,1)S(1)}, u32[]{:S(2)}, u32[]{:S(2)}) async-start(bf16[16,136,256]{2,1,0:T(8,128)(2,1)} %get-tuple-element.8), calls=%async_computation | async-start | bytes 2228224 | tf_op jit(solution)/shard_map/all_to_all | solution.py:216
  59.0 4.4 %copy-start.1 = (s32[2,16]{1,0:T(2,128)S(1)}, s32[2,16]{1,0:T(2,128)}, u32[]{:S(2)}) copy-start(s32[2,16]{1,0:T(2,128)} %param.9) | copy-start | bytes 388
  59.0 15.7 %all-to-all-start.1 = ((s16[4,136,1024]{2,1,0:T(8,128)(2,1)}), s16[4,136,1024]{2,1,0:T(8,128)(2,1)S(1)}, u32[]{:S(2)}, u32[]{:S(2)}) async-start(s16[4,136,1024]{2,1,0:T(8,128)(2,1)} %product.1), calls=%async_computation.1 | async-start | bytes 2228224 | tf_op jit(solution)/shard_map/all_to_all | solution.py:228

commit v5 on v4

--- a/solution.py
+++ b/solution.py
@@ -69,21 +69,23 @@
 
 
 def pack_kernel(a_mask, b_mask, at, b, a_out, b_out, a_bits, b_bits, a_in, b_in, a_packed, b_packed, sems):
+    pairs = (
+        (b_mask, b_bits),
+        (b.at[0], b_in.at[0]),
+        (a_mask, a_bits),
+        (at, a_in),
+        (b.at[1], b_in.at[1]),
+    )
     loads = [
         pltpu.make_async_copy(source, target, sems.at[n])
-        for n, (source, target) in enumerate(((b_mask, b_bits), (b, b_in), (a_mask, a_bits), (at, a_in)))
+        for n, (source, target) in enumerate(pairs)
     ]
-    for load in loads:
-        load.start()
+    for n in (0, 1, 4, 2, 3):
+        loads[n].start()
     row = lax.broadcasted_iota(I32, (EXTRA, 128), 0)
 
     loads[0].wait()
     ids = [slot_ids([b_bits[s, j] for j in range(BC)], MOSTB) for s in range(STEPS)]
-    loads[1].wait()
-    for s in range(STEPS):
-        pair = compact(lambda p: b_in[s, :, 128 * p : 128 * p + 128], BC // 2, ids[s])
-        for o in range(2):
-            b_packed[BS * s : BS * s + BS, 128 * o : 128 * o + 128] = pair[o]
     for o in range(2):
         index = jnp.where(
             row == 0,
@@ -91,9 +93,17 @@
             halves(ids[1][2 * o], ids[1][2 * o + 1], EXTRA),
         )
         b_packed[128 : 128 + EXTRA, 128 * o : 128 * o + 128] = narrow(index)
-    stores = [pltpu.make_async_copy(b_packed, b_out.at[d], sems.at[5 + d]) for d in range(KB)]
-    for store in stores:
-        store.start()
+    stores = []
+    for s in range(STEPS):
+        loads[(1, 4)[s]].wait()
+        pair = compact(lambda p: b_in[s, :, 128 * p : 128 * p + 128], BC // 2, ids[s])
+        for o in range(2):
+            b_packed[BS * s : BS * s + BS, 128 * o : 128 * o + 128] = pair[o]
+        here = pl.ds(BS * s, BS + EXTRA * s)
+        for d in range(KB):
+            sem = sems.at[6 + KB * s + d]
+            stores.append(pltpu.make_async_copy(b_packed.at[here], b_out.at[d, here], sem))
+            stores[-1].start()
 
     loads[2].wait()
     ids = [slot_ids([a_bits[s, i] for i in range(BR)], MOSTA) for s in range(STEPS)]
@@ -109,7 +119,7 @@
         halves(ids[0][1], ids[1][1], EXTRA),
     )
     a_packed[128 : 128 + EXTRA, :] = narrow(index)
-    stores.append(pltpu.make_async_copy(a_packed, a_out, sems.at[4]))
+    stores.append(pltpu.make_async_copy(a_packed, a_out, sems.at[5]))
     stores[-1].start()
     for store in stores:
         store.wait()
@@ -139,13 +149,13 @@
 def product_kernel(a, b, out):
     columns = []
     for c in range(KB):
-        index = a[c, 128 : 128 + EXTRA, :].astype(F32)
+        index = a[128 : 128 + EXTRA, 128 * c : 128 * c + 128].astype(F32)
         ids = [jnp.broadcast_to(index[s : s + 1], (BS, 128)).astype(BF16) for s in range(MOSTA)]
         blocks = []
         for i in range(BR):
             dense = jnp.zeros((BS, 128), BF16)
             for s in range(MOSTA):
-                dense = jnp.where(ids[s] == jnp.bfloat16(i), a[c, BS * s : BS * s + BS, :], dense)
+                dense = jnp.where(ids[s] == jnp.bfloat16(i), a[BS * s : BS * s + BS, 128 * c : 128 * c + 128], dense)
             blocks.append(dense)
         columns.append(jnp.concatenate(blocks, axis=0))
     left = jnp.concatenate(columns, axis=1)
@@ -203,7 +213,7 @@
             pltpu.VMEM((STEPS, BS, BC * BS), BF16),
             pltpu.VMEM((rows, 128), BF16),
             pltpu.VMEM((rows, 256), BF16),
-            pltpu.SemaphoreType.DMA((5 + KB,)),
+            pltpu.SemaphoreType.DMA((6 + STEPS * KB,)),
         ],
         cost_estimate=pl.CostEstimate(flops=10**6, bytes_accessed=2 * 10**6, transcendentals=0),
         name="pack",
@@ -214,7 +224,7 @@
         b_panel,
     )
     b_all = lax.all_to_all(b_sent, "row", 0, 0, tiled=True)
-    a_all = lax.all_gather(a_sent, "col")
+    a_all = lax.all_gather(a_sent, "col", axis=1, tiled=True)
     keep = jnp.repeat(c_pattern.astype(F32), BS, axis=1)
     sums = pl.pallas_call(
         product_kernel,

time: 75.9 us -> 76 us (level)
  no operation moved by 1% of the time
where the time goes in v5:
time: 76 us; the launch traced here: 75.7 us
  blocking collectives  36.5 us (48%)
  starting transfers between devices  21 us (28%)
  waiting for transfers between devices  11.1 us (15%)
  Pallas kernels  6.94 us (9%)
    all_gather x1, blocking collectives, body(): a_all = lax.all_gather(a_sent, 'col', axis=1, tiled=True)  36.5 us
    all_to_all x1, starting transfers between devices, body(): b_all = lax.all_to_all(b_sent, 'row', 0, 0, tiled=True)  16.6 us
    all_to_all x1, waiting for transfers between devices, body(): parts = lax.all_to_all(sums, 'layer', 0, 0, tiled=True)  11.1 us
    all_to_all x1, starting transfers between devices, body(): parts = lax.all_to_all(sums, 'layer', 0, 0, tiled=True)  4.42 us
    pallas_call x1, Pallas kernels, body(): pl.pallas_call(product_kernel, out_shape=jax.ShapeDtypeStruct((LAYERS, 12...  3.61 us
    pallas_call x1, Pallas kernels, body(): pl.pallas_call(pack_kernel, out_shape=(jax.ShapeDtypeStruct((rows, 128),...  2.36 us
  transfers between devices with their start and end apart: 2, of which 1 were waited for; matrix products, arithmetic and copies ran while one was open for 0% of the time, Pallas kernels for 0%

profile of v5, /device:TPU:8, one launch (start us, length us, event | category | flops | bytes accessed | tf_op | source)
XLA Modules:
  0.0 75.7 jit_solution(142913613620321419)
XLA Ops:
  0.0 2.4 %pack.1 = (bf16[136,128]{1,0:T(8,128)(2,1)}, bf16[16,136,256]{2,1,0:T(8,128)(2,1)}) custom-call(s32[2,8]{1,0:T(2,128)} %bitcast.4, s32[2,16]{1,0:T(2,128)} %bitcast.5, bf16[2,64,512]{2,1,0:T(8,128)(2,1)} %bitcast.3, bf16[2,64,1024]{2,1,0:T(8,128)(2,1)} %b.1), custom_call_target="tpu_custom_call" | custom-call | flops 1000000 | bytes 2000000 | tf_op jit(solution)/shard_map/pack/pallas_call | solution.py:201
  2.4 0.0 copy-start
  2.4 16.6 %all-to-all-start = ((bf16[16,136,256]{2,1,0:T(8,128)(2,1)}), bf16[16,136,256]{2,1,0:T(8,128)(2,1)S(1)}, u32[]{:S(2)}, u32[]{:S(2)}) async-start(bf16[16,136,256]{2,1,0:T(8,128)(2,1)} %get-tuple-element.8), calls=%async_computation | async-start | bytes 2228224 | tf_op jit(solution)/shard_map/all_to_all | solution.py:226
  19.0 0.0 copy-done
  19.0 36.5 %all_gather.3.a = bf16[136,2048]{1,0:T(8,128)(2,1)S(1)} all-gather(bf16[136,128]{1,0:T(8,128)(2,1)S(1)} %copy-done), channel_id=1, replica_groups=mesh['row'=16,'col'=16,'layer'=4] {'col'}, dimensions={1}, use_global_device_ids=true | all-gather | bytes 591872 | tf_op jit(solution)/shard_map/all_gather | solution.py:227
  55.4 0.0 all-to-all-done.b
  55.4 3.6 %product.1 = s16[4,136,1024]{2,1,0:T(8,128)(2,1)} custom-call(bf16[136,2048]{1,0:T(8,128)(2,1)S(1)} %all_gather.3.a, bf16[16,136,256]{2,1,0:T(8,128)(2,1)S(1)} %all-to-all-done.b), custom_call_target="tpu_custom_call" | custom-call | flops 2000000000 | bytes 6000000 | tf_op jit(solution)/shard_map/product/pallas_call | solution.py:229
  59.0 0.0 copy-start.1
  59.0 4.4 %all-to-all-start.1 = ((s16[4,136,1024]{2,1,0:T(8,128)(2,1)}), s16[4,136,1024]{2,1,0:T(8,128)(2,1)S(1)}, u32[]{:S(2)}, u32[]{:S(2)}) async-start(s16[4,136,1024]{2,1,0:T(8,128)(2,1)} %product.1), calls=%async_computation.1 | async-start | bytes 2228224 | tf_op jit(solution)/shard_map/all_to_all | solution.py:238
  63.5 0.0 copy-done.1
  63.5 0.1 broadcast_in_dim.3
  63.5 0.1 reshape.11.keep
  63.6 11.1 %all-to-all-done.1.parts = s16[4,136,1024]{2,1,0:T(8,128)(2,1)S(1)} async-done(((s16[4,136,1024]{2,1,0:T(8,128)(2,1)}), s16[4,136,1024]{2,1,0:T(8,128)(2,1)S(1)}, u32[]{:S(2)}, u32[]{:S(2)}) %all-to-all-start.1) | async-done | bytes 1114144 | tf_op jit(solution)/shard_map/all_to_all | solution.py:238
  74.7 1.0 %filter.1 = f32[128,1024]{1,0:T(8,128)} custom-call(s16[4,136,1024]{2,1,0:T(8,128)(2,1)S(1)} %all-to-all-done.1.parts, f32[2,1024]{1,0:T(2,128)S(1)} %reshape.11.keep), custom_call_target="tpu_custom_call" | custom-call | flops 1000000 | bytes 2000000 | tf_op jit(solution)/shard_map/filter/pallas_call | solution.py:239
  (1 shorter events, 0.0 us)
Async XLA Ops:
  2.4 16.6 %copy-start = (bf16[136,128]{1,0:T(8,128)(2,1)S(1)}, bf16[136,128]{1,0:T(8,128)(2,1)}, u32[]{:S(2)}) copy-start(bf16[136,128]{1,0:T(8,128)(2,1)} %get-tuple-element.7) | copy-start | bytes 104452
  2.4 53.1 %all-to-all-start = ((bf16[16,136,256]{2,1,0:T(8,128)(2,1)}), bf16[16,136,256]{2,1,0:T(8,128)(2,1)S(1)}, u32[]{:S(2)}, u32[]{:S(2)}) async-start(bf16[16,136,256]{2,1,0:T(8,128)(2,1)} %get-tuple-element.8), calls=%async_computation | async-start | bytes 2228224 | tf_op jit(solution)/shard_map/all_to_all | solution.py:226
  59.0 4.4 %copy-start.1 = (s32[2,16]{1,0:T(2,128)S(1)}, s32[2,16]{1,0:T(2,128)}, u32[]{:S(2)}) copy-start(s32[2,16]{1,0:T(2,128)} %param.9) | copy-start | bytes 388
  59.0 15.7 %all-to-all-start.1 = ((s16[4,136,1024]{2,1,0:T(8,128)(2,1)}), s16[4,136,1024]{2,1,0:T(8,128)(2,1)S(1)}, u32[]{:S(2)}, u32[]{:S(2)}) async-start(s16[4,136,1024]{2,1,0:T(8,128)(2,1)} %product.1), calls=%async_computation.1 | async-start | bytes 2228224 | tf_op jit(solution)/shard_map/all_to_all | solution.py:238

commit v6 on v4

--- a/solution.py
+++ b/solution.py
@@ -136,7 +136,7 @@
     return dense
 
 
-def product_kernel(a, b, out):
+def product_kernel(a, b, sent, out, sems):
     columns = []
     for c in range(KB):
         index = a[c, 128 : 128 + EXTRA, :].astype(F32)
@@ -152,6 +152,7 @@
     turned = {(k, s): turn(b, k, s) for k in range(KB) for s in range(STEPS)}
     rows = out.shape[1] - EXTRA
     tiles, width = 2, 512
+    stores = []
     for t in range(tiles):
         cols = slice(width * t, width * t + width)
         dense = []
@@ -167,6 +168,11 @@
             out[l, 0:rows, cols] = jnp.round(part * jnp.exp2(-power)).astype(I32).astype(I16)
             power = jnp.broadcast_to(power, (EXTRA, width))
             out[l, rows : rows + EXTRA, cols] = power.astype(I32).astype(I16)
+        here = pl.ds(width * t, width)
+        stores.append(pltpu.make_async_copy(out.at[:, :, here], sent.at[:, :, here], sems.at[t]))
+        stores[-1].start()
+    for store in stores:
+        store.wait()
 
 
 def filter_kernel(parts, keep, out, total, sems):
@@ -220,7 +226,11 @@
         product_kernel,
         out_shape=jax.ShapeDtypeStruct((LAYERS, 128 + EXTRA, 1024), I16),
         in_specs=[VMEM, VMEM],
-        out_specs=VMEM,
+        out_specs=ANY,
+        scratch_shapes=[
+            pltpu.VMEM((LAYERS, 128 + EXTRA, 1024), I16),
+            pltpu.SemaphoreType.DMA((2,)),
+        ],
         cost_estimate=pl.CostEstimate(flops=2 * 10**9, bytes_accessed=6 * 10**6, transcendentals=0),
         compiler_params=grant(24),
         name="product",

time: 75.9 us -> 75.7 us (level)
  no operation moved by 1% of the time
where the time goes in v6:
time: 75.7 us; the launch traced here: 75.4 us
  blocking collectives  36.5 us (48%)
  starting transfers between devices  20.9 us (28%)
  waiting for transfers between devices  11.1 us (15%)
  Pallas kernels  6.74 us (9%)
    all_gather x1, blocking collectives, body(): a_all = lax.all_gather(a_sent, 'col')  36.5 us
    all_to_all x1, starting transfers between devices, body(): b_all = lax.all_to_all(b_sent, 'row', 0, 0, tiled=True)  16.6 us
    all_to_all x1, waiting for transfers between devices, body(): parts = lax.all_to_all(sums, 'layer', 0, 0, tiled=True)  11.1 us
    all_to_all x1, starting transfers between devices, body(): parts = lax.all_to_all(sums, 'layer', 0, 0, tiled=True)  4.3 us
    pallas_call x1, Pallas kernels, body(): pl.pallas_call(product_kernel, out_shape=jax.ShapeDtypeStruct((LAYERS, 12...  3.48 us
    pallas_call x1, Pallas kernels, body(): pl.pallas_call(pack_kernel, out_shape=(jax.ShapeDtypeStruct((rows, 128),...  2.28 us
  transfers between devices with their start and end apart: 2, of which 1 were waited for; matrix products, arithmetic and copies ran while one was open for 0% of the time, Pallas kernels for 0%

profile of v6, /device:TPU:8, one launch (start us, length us, event | category | flops | bytes accessed | tf_op | source)
XLA Modules:
  0.0 75.4 jit_solution(17649037195896849797)
XLA Ops:
  0.0 2.3 %pack.1 = (bf16[136,128]{1,0:T(8,128)(2,1)}, bf16[16,136,256]{2,1,0:T(8,128)(2,1)}) custom-call(s32[2,8]{1,0:T(2,128)} %bitcast.6, s32[2,16]{1,0:T(2,128)} %bitcast.7, bf16[2,64,512]{2,1,0:T(8,128)(2,1)} %bitcast.5, bf16[2,64,1024]{2,1,0:T(8,128)(2,1)} %b.1), custom_call_target="tpu_custom_call" | custom-call | flops 1000000 | bytes 2000000 | tf_op jit(solution)/shard_map/pack/pallas_call | solution.py:197
  2.3 0.0 copy-start
  2.3 16.6 %all-to-all-start = ((bf16[16,136,256]{2,1,0:T(8,128)(2,1)}), bf16[16,136,256]{2,1,0:T(8,128)(2,1)S(1)}, u32[]{:S(2)}, u32[]{:S(2)}) async-start(bf16[16,136,256]{2,1,0:T(8,128)(2,1)} %get-tuple-element.8), calls=%async_computation | async-start | bytes 2228224 | tf_op jit(solution)/shard_map/all_to_all | solution.py:222
  18.9 0.0 copy-done
  18.9 36.5 %all-gather = bf16[2176,128]{1,0:T(8,128)(2,1)S(1)} all-gather(bf16[136,128]{1,0:T(8,128)(2,1)S(1)} %copy-done), channel_id=2, replica_groups=mesh['row'=16,'col'=16,'layer'=4] {'col'}, dimensions={0}, use_global_device_ids=true | all-gather | bytes 591872 | tf_op jit(solution)/shard_map/all_gather | solution.py:223
  55.4 0.0 all-to-all-done.b
  55.4 3.5 %product.1 = s16[4,136,1024]{2,1,0:T(8,128)(2,1)} custom-call(bf16[16,136,128]{2,1,0:T(8,128)(2,1)S(1)} %bitcast.4, bf16[16,136,256]{2,1,0:T(8,128)(2,1)S(1)} %all-to-all-done.b), custom_call_target="tpu_custom_call" | custom-call | flops 2000000000 | bytes 6000000 | tf_op jit(solution)/shard_map/product/pallas_call | solution.py:225
  58.9 0.0 copy-start.1
  58.9 4.3 %all-to-all-start.1 = ((s16[4,136,1024]{2,1,0:T(8,128)(2,1)}), s16[4,136,1024]{2,1,0:T(8,128)(2,1)S(1)}, u32[]{:S(2)}, u32[]{:S(2)}) async-start(s16[4,136,1024]{2,1,0:T(8,128)(2,1)} %product.1), calls=%async_computation.1 | async-start | bytes 2228224 | tf_op jit(solution)/shard_map/all_to_all | solution.py:238
  63.2 0.0 copy-done.1
  63.2 0.1 broadcast_in_dim.3
  63.3 0.1 reshape.11.keep
  63.3 11.1 %all-to-all-done.1.parts = s16[4,136,1024]{2,1,0:T(8,128)(2,1)S(1)} async-done(((s16[4,136,1024]{2,1,0:T(8,128)(2,1)}), s16[4,136,1024]{2,1,0:T(8,128)(2,1)S(1)}, u32[]{:S(2)}, u32[]{:S(2)}) %all-to-all-start.1) | async-done | bytes 1114144 | tf_op jit(solution)/shard_map/all_to_all | solution.py:238
  74.4 1.0 %filter.1 = f32[128,1024]{1,0:T(8,128)} custom-call(s16[4,136,1024]{2,1,0:T(8,128)(2,1)S(1)} %all-to-all-done.1.parts, f32[2,1024]{1,0:T(2,128)S(1)} %reshape.11.keep), custom_call_target="tpu_custom_call" | custom-call | flops 1000000 | bytes 2000000 | tf_op jit(solution)/shard_map/filter/pallas_call | solution.py:239
  (1 shorter events, 0.0 us)
Async XLA Ops:
  2.3 16.6 %copy-start = (bf16[136,128]{1,0:T(8,128)(2,1)S(1)}, bf16[136,128]{1,0:T(8,128)(2,1)}, u32[]{:S(2)}) copy-start(bf16[136,128]{1,0:T(8,128)(2,1)} %get-tuple-element.7) | copy-start | bytes 104452
  2.3 53.1 %all-to-all-start = ((bf16[16,136,256]{2,1,0:T(8,128)(2,1)}), bf16[16,136,256]{2,1,0:T(8,128)(2,1)S(1)}, u32[]{:S(2)}, u32[]{:S(2)}) async-start(bf16[16,136,256]{2,1,0:T(8,128)(2,1)} %get-tuple-element.8), calls=%async_computation | async-start | bytes 2228224 | tf_op jit(solution)/shard_map/all_to_all | solution.py:222
  58.9 4.3 %copy-start.1 = (s32[2,16]{1,0:T(2,128)S(1)}, s32[2,16]{1,0:T(2,128)}, u32[]{:S(2)}) copy-start(s32[2,16]{1,0:T(2,128)} %param.9) | copy-start | bytes 388
  58.9 15.5 %all-to-all-start.1 = ((s16[4,136,1024]{2,1,0:T(8,128)(2,1)}), s16[4,136,1024]{2,1,0:T(8,128)(2,1)S(1)}, u32[]{:S(2)}, u32[]{:S(2)}) async-start(s16[4,136,1024]{2,1,0:T(8,128)(2,1)} %product.1), calls=%async_computation.1 | async-start | bytes 2228224 | tf_op jit(solution)/shard_map/all_to_all | solution.py:238

commit v7 on v5

--- a/solution.py
+++ b/solution.py
@@ -146,22 +146,23 @@
     return dense
 
 
-def product_kernel(a, b, out):
+def product_kernel(a, b, sent, out, sems):
     columns = []
     for c in range(KB):
-        index = a[128 : 128 + EXTRA, 128 * c : 128 * c + 128].astype(F32)
+        index = a[c, 128 : 128 + EXTRA, :].astype(F32)
         ids = [jnp.broadcast_to(index[s : s + 1], (BS, 128)).astype(BF16) for s in range(MOSTA)]
         blocks = []
         for i in range(BR):
             dense = jnp.zeros((BS, 128), BF16)
             for s in range(MOSTA):
-                dense = jnp.where(ids[s] == jnp.bfloat16(i), a[BS * s : BS * s + BS, 128 * c : 128 * c + 128], dense)
+                dense = jnp.where(ids[s] == jnp.bfloat16(i), a[c, BS * s : BS * s + BS, :], dense)
             blocks.append(dense)
         columns.append(jnp.concatenate(blocks, axis=0))
     left = jnp.concatenate(columns, axis=1)
     turned = {(k, s): turn(b, k, s) for k in range(KB) for s in range(STEPS)}
     rows = out.shape[1] - EXTRA
     tiles, width = 2, 512
+    stores = []
     for t in range(tiles):
         cols = slice(width * t, width * t + width)
         dense = []
@@ -177,6 +178,11 @@
             out[l, 0:rows, cols] = jnp.round(part * jnp.exp2(-power)).astype(I32).astype(I16)
             power = jnp.broadcast_to(power, (EXTRA, width))
             out[l, rows : rows + EXTRA, cols] = power.astype(I32).astype(I16)
+        here = pl.ds(width * t, width)
+        stores.append(pltpu.make_async_copy(out.at[:, :, here], sent.at[:, :, here], sems.at[t]))
+        stores[-1].start()
+    for store in stores:
+        store.wait()
 
 
 def filter_kernel(parts, keep, out, total, sems):
@@ -224,13 +230,17 @@
         b_panel,
     )
     b_all = lax.all_to_all(b_sent, "row", 0, 0, tiled=True)
-    a_all = lax.all_gather(a_sent, "col", axis=1, tiled=True)
+    a_all = lax.all_gather(a_sent, "col")
     keep = jnp.repeat(c_pattern.astype(F32), BS, axis=1)
     sums = pl.pallas_call(
         product_kernel,
         out_shape=jax.ShapeDtypeStruct((LAYERS, 128 + EXTRA, 1024), I16),
         in_specs=[VMEM, VMEM],
-        out_specs=VMEM,
+        out_specs=ANY,
+        scratch_shapes=[
+            pltpu.VMEM((LAYERS, 128 + EXTRA, 1024), I16),
+            pltpu.SemaphoreType.DMA((2,)),
+        ],
         cost_estimate=pl.CostEstimate(flops=2 * 10**9, bytes_accessed=6 * 10**6, transcendentals=0),
         compiler_params=grant(24),
         name="product",

time: 76 us -> 75.8 us (level)
  no operation moved by 1% of the time
where the time goes in v7:
time: 75.8 us; the launch traced here: 75.5 us
  blocking collectives  36.5 us (48%)
  starting transfers between devices  20.9 us (28%)
  waiting for transfers between devices  11.1 us (15%)
  Pallas kernels  6.82 us (9%)
    all_gather x1, blocking collectives, body(): a_all = lax.all_gather(a_sent, 'col')  36.5 us
    all_to_all x1, starting transfers between devices, body(): b_all = lax.all_to_all(b_sent, 'row', 0, 0, tiled=True)  16.6 us
    all_to_all x1, waiting for transfers between devices, body(): parts = lax.all_to_all(sums, 'layer', 0, 0, tiled=True)  11.1 us
    all_to_all x1, starting transfers between devices, body(): parts = lax.all_to_all(sums, 'layer', 0, 0, tiled=True)  4.3 us
    pallas_call x1, Pallas kernels, body(): pl.pallas_call(product_kernel, out_shape=jax.ShapeDtypeStruct((LAYERS, 12...  3.48 us
    pallas_call x1, Pallas kernels, body(): pl.pallas_call(pack_kernel, out_shape=(jax.ShapeDtypeStruct((rows, 128),...  2.36 us
  transfers between devices with their start and end apart: 2, of which 1 were waited for; matrix products, arithmetic and copies ran while one was open for 0% of the time, Pallas kernels for 0%

profile of v7, /device:TPU:8, one launch (start us, length us, event | category | flops | bytes accessed | tf_op | source)
XLA Modules:
  0.0 75.5 jit_solution(15999265271663396444)
XLA Ops:
  0.0 2.4 %pack.1 = (bf16[136,128]{1,0:T(8,128)(2,1)}, bf16[16,136,256]{2,1,0:T(8,128)(2,1)}) custom-call(s32[2,8]{1,0:T(2,128)} %bitcast.6, s32[2,16]{1,0:T(2,128)} %bitcast.7, bf16[2,64,512]{2,1,0:T(8,128)(2,1)} %bitcast.5, bf16[2,64,1024]{2,1,0:T(8,128)(2,1)} %b.1), custom_call_target="tpu_custom_call" | custom-call | flops 1000000 | bytes 2000000 | tf_op jit(solution)/shard_map/pack/pallas_call | solution.py:207
  2.4 0.0 copy-start
  2.4 16.6 %all-to-all-start = ((bf16[16,136,256]{2,1,0:T(8,128)(2,1)}), bf16[16,136,256]{2,1,0:T(8,128)(2,1)S(1)}, u32[]{:S(2)}, u32[]{:S(2)}) async-start(bf16[16,136,256]{2,1,0:T(8,128)(2,1)} %get-tuple-element.8), calls=%async_computation | async-start | bytes 2228224 | tf_op jit(solution)/shard_map/all_to_all | solution.py:232
  19.0 0.0 copy-done
  19.0 36.5 %all-gather = bf16[2176,128]{1,0:T(8,128)(2,1)S(1)} all-gather(bf16[136,128]{1,0:T(8,128)(2,1)S(1)} %copy-done), channel_id=2, replica_groups=mesh['row'=16,'col'=16,'layer'=4] {'col'}, dimensions={0}, use_global_device_ids=true | all-gather | bytes 591872 | tf_op jit(solution)/shard_map/all_gather | solution.py:233
  55.4 0.0 all-to-all-done.b
  55.4 3.5 %product.1 = s16[4,136,1024]{2,1,0:T(8,128)(2,1)} custom-call(bf16[16,136,128]{2,1,0:T(8,128)(2,1)S(1)} %bitcast.4, bf16[16,136,256]{2,1,0:T(8,128)(2,1)S(1)} %all-to-all-done.b), custom_call_target="tpu_custom_call" | custom-call | flops 2000000000 | bytes 6000000 | tf_op jit(solution)/shard_map/product/pallas_call | solution.py:235
  58.9 0.0 copy-start.1
  58.9 4.3 %all-to-all-start.1 = ((s16[4,136,1024]{2,1,0:T(8,128)(2,1)}), s16[4,136,1024]{2,1,0:T(8,128)(2,1)S(1)}, u32[]{:S(2)}, u32[]{:S(2)}) async-start(s16[4,136,1024]{2,1,0:T(8,128)(2,1)} %product.1), calls=%async_computation.1 | async-start | bytes 2228224 | tf_op jit(solution)/shard_map/all_to_all | solution.py:248
  63.2 0.0 copy-done.1
  63.3 0.1 broadcast_in_dim.3
  63.3 0.1 reshape.11.keep
  63.4 11.1 %all-to-all-done.1.parts = s16[4,136,1024]{2,1,0:T(8,128)(2,1)S(1)} async-done(((s16[4,136,1024]{2,1,0:T(8,128)(2,1)}), s16[4,136,1024]{2,1,0:T(8,128)(2,1)S(1)}, u32[]{:S(2)}, u32[]{:S(2)}) %all-to-all-start.1) | async-done | bytes 1114144 | tf_op jit(solution)/shard_map/all_to_all | solution.py:248
  74.5 1.0 %filter.1 = f32[128,1024]{1,0:T(8,128)} custom-call(s16[4,136,1024]{2,1,0:T(8,128)(2,1)S(1)} %all-to-all-done.1.parts, f32[2,1024]{1,0:T(2,128)S(1)} %reshape.11.keep), custom_call_target="tpu_custom_call" | custom-call | flops 1000000 | bytes 2000000 | tf_op jit(solution)/shard_map/filter/pallas_call | solution.py:249
  (1 shorter events, 0.0 us)
Async XLA Ops:
  2.4 16.6 %copy-start = (bf16[136,128]{1,0:T(8,128)(2,1)S(1)}, bf16[136,128]{1,0:T(8,128)(2,1)}, u32[]{:S(2)}) copy-start(bf16[136,128]{1,0:T(8,128)(2,1)} %get-tuple-element.7) | copy-start | bytes 104452
  2.4 53.1 %all-to-all-start = ((bf16[16,136,256]{2,1,0:T(8,128)(2,1)}), bf16[16,136,256]{2,1,0:T(8,128)(2,1)S(1)}, u32[]{:S(2)}, u32[]{:S(2)}) async-start(bf16[16,136,256]{2,1,0:T(8,128)(2,1)} %get-tuple-element.8), calls=%async_computation | async-start | bytes 2228224 | tf_op jit(solution)/shard_map/all_to_all | solution.py:232
  58.9 4.3 %copy-start.1 = (s32[2,16]{1,0:T(2,128)S(1)}, s32[2,16]{1,0:T(2,128)}, u32[]{:S(2)}) copy-start(s32[2,16]{1,0:T(2,128)} %param.9) | copy-start | bytes 388
  58.9 15.5 %all-to-all-start.1 = ((s16[4,136,1024]{2,1,0:T(8,128)(2,1)}), s16[4,136,1024]{2,1,0:T(8,128)(2,1)S(1)}, u32[]{:S(2)}, u32[]{:S(2)}) async-start(s16[4,136,1024]{2,1,0:T(8,128)(2,1)} %product.1), calls=%async_computation.1 | async-start | bytes 2228224 | tf_op jit(solution)/shard_map/all_to_all | solution.py:248
